TPU v7x, 128 devices: a whole 4x4x4 slice. The times are simulated.
128 devices in a mesh: blk: 16 (over z, y_lo, core), exp: 8 (over y_hi, x).
Axes of the slice: x: 4, y: 4 (y_hi: 2, y_lo: 2; y = y_hi * 2 + y_lo), z: 4, core: 2. Of those that a mesh axis runs over, the one named last changes fastest.
Arguments:
- nodes: bfloat16 [24576, 512], P('blk'), may hold values from -8 to 8
- attention_weights: bfloat16 [3, 256, 512], P(None, 'exp'), may hold values from -1.5 to 1.5
- output_weight: bfloat16 [256, 512], P('exp'), may hold values from -2 to 2
- router_weight: bfloat16 [8, 512], replicated, may hold values from -1.25 to 1.25
- gain_first: float32 [512], replicated, may hold values from 0.1 to 1.9
- gain_second: float32 [512], replicated, may hold values from 0.1 to 1.9
- expert_in: bfloat16 [8, 2048, 512], P('exp', 'blk'), may hold values from -0.25 to 0.25
- expert_out: bfloat16 [8, 2048, 512], P('exp', 'blk'), may hold values from -0.125 to 0.125
- routes: int32 [24576, 2], P(('blk', 'exp')), may hold values from 0 to 7, all different within a row; in each aligned block of 192 rows (0 to 191, 192 to 383, ...) at most 96 rows name the same one
- cotangent: bfloat16 [24576, 512], P(('blk', 'exp')), may hold values from -6 to 6
Outputs:
- layer_out: bfloat16 [24576, 512], P(('blk', 'exp'))
- stream_grad: bfloat16 [24576, 512], P(('blk', 'exp'))
- expert_in_grad: float32 [8, 2048, 512], P('exp', 'blk')
- expert_out_grad: float32 [8, 2048, 512], P('exp', 'blk')
- router_grad: float32 [8, 512], replicated
- gain_grad: float32 [512], replicated
Inputs may be any that keep to these rules, and one draw needn't show every extreme that they name: `routes`: each row names two different experts. Among the rows of one device (aligned blocks of 192 rows) no expert is named by more than 96 rows, and in some block one expert is named by exactly 96 rows.
All inputs are finite; a program needn't handle non-finite values.
Results may differ from a plain program's by a relative error of at most 0.04.
The roundings to bfloat16 on the way count: a program that leaves them out, or rounds other values in their place, can miss the bound.
Values may be sent and summed in bfloat16 or wider, within the bound.
No kernel may reach another device: no remote copies, remote signals or barrier semaphores. Data moves between devices by JAX's collectives and lax.ppermute only.
A program may use at most 64 MiB of HBM per device.

v0:
```python
import math

import jax
import jax.numpy as jnp
from jax import lax
from jax.experimental import pallas as pl
from jax.experimental.pallas import tpu as pltpu
from jax.sharding import PartitionSpec as P

HD = 32

EPSILON = 1e-06
LOG2_SCALE = math.log2(math.e) / math.sqrt(HD)
SHIFT_KEYS = 256
SUM_LIMIT = 2.0**100
ATTENTION_VMEM = 40 * 2**20
EXPERT_VMEM = 24 * 2**20
SUM_ROWS = 16
TANH_SCALE = math.sqrt(2.0 / math.pi)
CUBE = 0.044715


def rms_gain(stream, gain):
    return stream * lax.rsqrt(jnp.mean(stream * stream, axis=-1, keepdims=True) + EPSILON) * gain


def exchange(buffer):
    return lax.all_to_all(buffer, "exp", split_axis=0, concat_axis=0, tiled=True)


def hop(value, axis, target):
    count = lax.axis_size(axis)
    return lax.ppermute(value, axis, [(i, target(i) % count) for i in range(count)])


def split_terms(value, terms):
    pieces = []
    for _ in range(terms):
        piece = value.astype(jnp.bfloat16)
        pieces.append(piece)
        value = value - piece.astype(jnp.float32)
    return pieces


def key_blocks(refs):
    return [
        (ref, start) for ref in refs for start in range(0, ref.shape[0], 2 * HD)
    ]


def own_blocks(own_ref):
    return [(own_ref, HD)]


def load_keys(blocks, keys, values):
    width = blocks[0][0].shape[1]
    ones = (lax.broadcasted_iota(jnp.int32, (HD, width), 0) < 3).astype(jnp.bfloat16)
    one = (lax.broadcasted_iota(jnp.int32, (HD // 2, width), 0) < 1).astype(jnp.bfloat16)
    for index, (ref, start) in enumerate(blocks):
        block = ref[start : start + HD, :]
        span = slice(index * width, (index + 1) * width)
        keys[span, :] = jnp.concatenate([block, block, block, ones], axis=0).T
        values[:, span] = jnp.concatenate([ref[start + HD : start + 2 * HD, :], one], axis=0)


def add_blocks(count, width, query, keys, values, total):
    chunk = width // 2

    def step(index, running):
        span = pl.ds(pl.multiple_of(index * chunk, chunk), chunk)
        exponents = jnp.dot(keys[span, :], query, preferred_element_type=jnp.float32)
        weights = jnp.exp2(exponents).astype(jnp.bfloat16)
        return running + jnp.dot(values[:, span], weights, preferred_element_type=jnp.float32)

    return lax.fori_loop(0, 2 * count, step, total)


def first_keys_kernel(count, own_ref, *refs):
    blocks, (wide_ref, total_ref, keys, values) = refs[:-4], refs[-4:]
    load_keys(own_blocks(own_ref) + key_blocks(blocks), keys, values)
    width = own_ref.shape[1]
    scaled = own_ref[:HD, :].astype(jnp.float32) * LOG2_SCALE
    pieces = split_terms(scaled, 3)
    wide_ref[...] = jnp.concatenate(pieces + [jnp.zeros_like(pieces[0])], axis=0)
    some = jnp.dot(keys[:SHIFT_KEYS, :], wide_ref[...], preferred_element_type=jnp.float32)
    shift = split_terms(-jnp.max(some, axis=0, keepdims=True), 3)
    row = lax.broadcasted_iota(jnp.int32, (HD, width), 0)
    rows = jnp.zeros((HD, width), jnp.float32)
    for index, piece in enumerate(shift):
        rows = jnp.where(row == index, piece.astype(jnp.float32), rows)
    wide_ref[3 * HD :, :] = rows.astype(jnp.bfloat16)
    total_ref[...] = add_blocks(
        count, width, wide_ref[...], keys, values, jnp.zeros(total_ref.shape, jnp.float32)
    )


def more_keys_kernel(count, wide_ref, before_ref, *refs):
    blocks, (total_ref, keys, values) = refs[:-3], refs[-3:]
    load_keys(key_blocks(blocks), keys, values)
    total_ref[...] = add_blocks(
        count, wide_ref.shape[1], wide_ref[...], keys, values, before_ref[...]
    )


def last_keys_kernel(count, fresh, wide_ref, before_ref, own_ref, output_weight_ref, *refs):
    blocks, (out_ref, keys, values, total) = refs[:-4], refs[-4:]
    load_keys(key_blocks(blocks[:fresh]), keys, values)
    width = wide_ref.shape[1]
    total[...] = add_blocks(count, width, wide_ref[...], keys, values, before_ref[...])
    sums = total[HD : HD + 1, :]
    inside = jnp.logical_and(sums <= SUM_LIMIT, sums >= 1.0 / SUM_LIMIT)
    outside = jnp.sum(jnp.where(inside, 0, 1))

    @pl.when(outside > 0)
    def _():
        query = own_ref[:HD, :]
        query = jnp.concatenate([query, jnp.zeros((3 * HD, width), query.dtype)], axis=0)
        total[...] = jnp.zeros(total.shape, jnp.float32)

        def step(index, top):
            span = pl.ds(pl.multiple_of(index * SHIFT_KEYS, SHIFT_KEYS), SHIFT_KEYS)
            scores = LOG2_SCALE * jnp.dot(
                keys[span, :], query, preferred_element_type=jnp.float32
            )
            new_top = jnp.maximum(top, jnp.max(scores, axis=0, keepdims=True))
            weights = jnp.exp2(scores - new_top).astype(jnp.bfloat16)
            total[...] = total[...] * jnp.exp2(top - new_top) + jnp.dot(
                values[:, span], weights, preferred_element_type=jnp.float32
            )
            return new_top

        top = jnp.full((1, width), -1e30, jnp.float32)
        every = own_blocks(own_ref) + key_blocks(blocks)
        for group in [every[i : i + count] for i in range(0, len(every), count)]:
            load_keys(group, keys, values)
            top = lax.fori_loop(0, len(group) * (width // SHIFT_KEYS), step, top)

    attended = (total[:HD, :] / total[HD : HD + 1, :]).astype(jnp.bfloat16)
    weight = output_weight_ref[...]
    features = weight.shape[1]
    rows = out_ref.shape[2] - features
    for index in range(out_ref.shape[0]):
        out_ref[index, :, :features] = weight
        out_ref[index, :, features:] = attended[:, index * rows : (index + 1) * rows]


def block_count(arrays):
    return sum(array.shape[0] for array in arrays) // (2 * HD)


def attention_call(kernel, out_shape, operands, count, width, extra=(), aliases=None):
    specs = [pl.BlockSpec(memory_space=pltpu.VMEM)]
    return pl.pallas_call(
        kernel,
        out_shape=out_shape,
        in_specs=specs * len(operands),
        out_specs=jax.tree.map(lambda _: specs[0], out_shape),
        scratch_shapes=[
            pltpu.VMEM((count * width, 4 * HD), jnp.bfloat16),
            pltpu.VMEM((HD + HD // 2, count * width), jnp.bfloat16),
            *extra,
        ],
        input_output_aliases=aliases or {},
        compiler_params=pltpu.CompilerParams(vmem_limit_bytes=ATTENTION_VMEM),
        cost_estimate=pl.CostEstimate(
            flops=count * width * width * 1200,
            transcendentals=count * width * width,
            bytes_accessed=count * width * 4 * HD,
        ),
    )(*operands)


def near_hops(value):
    return [hop(value, "blk", lambda i, step=step: i ^ step) for step in (2, 4, 12, 8)]


def attention(projected, output_weight, expert_weights, owners):
    width = projected.shape[1]
    keys_values = projected[HD:]
    partner = hop(keys_values, "blk", lambda i: i ^ 1)
    near = near_hops(keys_values)
    total_shape = jax.ShapeDtypeStruct((HD + HD // 2, width), jnp.float32)
    wide_shape = jax.ShapeDtypeStruct((4 * HD, width), jnp.bfloat16)
    wide, total = attention_call(
        lambda *refs: first_keys_kernel(2, *refs),
        (wide_shape, total_shape),
        [projected, partner],
        2,
        width,
    )

    def more(total, group):
        count = block_count(group)
        return attention_call(
            lambda *refs: more_keys_kernel(count, *refs),
            total_shape,
            [wide, total, *group],
            count,
            width,
            aliases={1: 0},
        )

    near, total = lax.optimization_barrier((near, total))
    beyond = hop(jnp.concatenate(near[1:], axis=0), "blk", lambda i: i ^ 2)
    near_partner = hop(jnp.concatenate(near, axis=0), "blk", lambda i: i ^ 1)
    total = more(total, near)
    near_partner, expert_weights, total = lax.optimization_barrier(
        (near_partner, expert_weights, total)
    )
    beside = hop(expert_weights, "blk", lambda i: i ^ 2)
    total = more(total, [near_partner])
    beyond, beside, total = lax.optimization_barrier((beyond, beside, total))
    beyond_partner = hop(beyond, "blk", lambda i: i ^ 1)
    pair = jnp.stack([expert_weights, beside])
    lane = [pair, *[hop(pair, "blk", lambda i, step=step: i ^ step) for step in (4, 8, 12)]]
    total = more(total, [beyond])
    beyond_partner, total = lax.optimization_barrier((beyond_partner, total))
    last = [beyond_partner]
    count = block_count(last)
    features = output_weight.shape[1]
    attended = attention_call(
        lambda *refs: last_keys_kernel(count, len(last), *refs),
        jax.ShapeDtypeStruct((owners, HD, features + width // owners), jnp.bfloat16),
        [wide, total, projected, output_weight, *last, partner, *near, near_partner, beyond],
        count,
        width,
        extra=[pltpu.VMEM(total_shape.shape, jnp.float32)],
    )
    return attended, lane


def add_rows(block, rows):
    return jnp.concatenate([block.reshape(-1, block.shape[-1]), rows], axis=0)


def dot_rows(first, second):
    return lax.dot_general(
        first, second, (((1,), (1,)), ((), ())), preferred_element_type=jnp.float32
    )


def tanh_part(values):
    return jnp.tanh(TANH_SCALE * (values + CUBE * (values * values * values)))


def tile_rows(lane_ref, partner_ref):
    share, width = lane_ref.shape[1:]
    return jnp.concatenate(
        [ref[...].reshape(2 * share, width) for ref in (lane_ref, partner_ref)], axis=0
    )


def weight_specs(weights):
    _, _, _, share, width = weights.shape
    return [
        pl.BlockSpec((None, 2, None, share, width), lambda i, which=which: (i, 0, which, 0, 0))
        for which in (0, 0, 1, 1)
    ]


def expert_forward_kernel(rows_ref, in_lane, in_partner, out_lane, out_partner, result_ref, total):
    step = pl.program_id(0)
    pre_act = dot_rows(rows_ref[...], tile_rows(in_lane, in_partner))
    hidden = (pre_act * (0.5 * (1.0 + tanh_part(pre_act)))).astype(jnp.bfloat16)
    part = jnp.dot(
        hidden, tile_rows(out_lane, out_partner), preferred_element_type=jnp.float32
    )

    @pl.when(step == 0)
    def _():
        total[...] = part

    @pl.when(step > 0)
    def _():
        total[...] += part

    @pl.when(step == pl.num_programs(0) - 1)
    def _():
        result_ref[...] = total[...].astype(result_ref.dtype)


def expert_forward(rows, lane, partner):
    count, width = rows.shape
    hidden = lane.size // width
    return pl.pallas_call(
        expert_forward_kernel,
        grid=(lane.shape[0],),
        out_shape=jax.ShapeDtypeStruct((count, width), jnp.bfloat16),
        in_specs=[pl.BlockSpec((count, width), lambda i: (0, 0)), *weight_specs(lane)],
        out_specs=pl.BlockSpec((count, width), lambda i: (0, 0)),
        scratch_shapes=[pltpu.VMEM((count, width), jnp.float32)],
        compiler_params=pltpu.CompilerParams(vmem_limit_bytes=EXPERT_VMEM),
        cost_estimate=pl.CostEstimate(
            flops=4 * count * width * hidden,
            transcendentals=count * hidden,
            bytes_accessed=4 * hidden * width,
        ),
    )(rows, lane, partner, lane, partner)


def expert_slopes_kernel(
    rows_ref,
    in_lane,
    in_partner,
    out_lane,
    out_partner,
    hidden_ref,
    slope_ref,
    out_weight_ref,
    in_weight_ref,
):
    weight_in = tile_rows(in_lane, in_partner)
    out_weight_ref[...] = tile_rows(out_lane, out_partner)
    in_weight_ref[...] = weight_in.T
    pre_act = dot_rows(weight_in, rows_ref[...])
    tanh = tanh_part(pre_act)
    half = 0.5 * (1.0 + tanh)
    hidden_ref[...] = (pre_act * half).astype(hidden_ref.dtype)
    slope_ref[...] = half + pre_act * (0.5 * (1.0 - tanh * tanh)) * (
        TANH_SCALE * (1.0 + 3.0 * CUBE * (pre_act * pre_act))
    )


def expert_slopes(rows, lane, partner):
    count, width = rows.shape
    hidden = lane.size // width
    tile = hidden // lane.shape[0]
    return pl.pallas_call(
        expert_slopes_kernel,
        grid=(lane.shape[0],),
        out_shape=(
            jax.ShapeDtypeStruct((hidden, count), jnp.bfloat16),
            jax.ShapeDtypeStruct((hidden, count), jnp.float32),
            jax.ShapeDtypeStruct((hidden, width), jnp.bfloat16),
            jax.ShapeDtypeStruct((width, hidden), jnp.bfloat16),
        ),
        in_specs=[pl.BlockSpec((count, width), lambda i: (0, 0)), *weight_specs(lane)],
        out_specs=(
            pl.BlockSpec((tile, count), lambda i: (i, 0)),
            pl.BlockSpec((tile, count), lambda i: (i, 0)),
            pl.BlockSpec((tile, width), lambda i: (i, 0)),
            pl.BlockSpec((width, tile), lambda i: (0, i)),
        ),
        compiler_params=pltpu.CompilerParams(vmem_limit_bytes=EXPERT_VMEM),
        cost_estimate=pl.CostEstimate(
            flops=2 * count * width * hidden,
            transcendentals=count * hidden,
            bytes_accessed=6 * count * hidden + 8 * hidden * width,
        ),
    )(rows, lane, partner, lane, partner)


def store_shares(term, mine_ref, theirs_ref):
    share = mine_ref.shape[2]
    for y in range(2):
        mine_ref[0, y] = term[y * share : (y + 1) * share]
        theirs_ref[0, y] = term[(y + 2) * share : (y + 3) * share].astype(theirs_ref.dtype)


def routed_rows(grads_ref):
    sources, rows, width = grads_ref.shape
    rows = rows - SUM_ROWS
    return grads_ref[:, :rows, :].reshape(sources * rows, width)


def expert_out_grad_kernel(scale, hidden_ref, grads_ref, mine_ref, theirs_ref):
    term = jnp.dot(hidden_ref[...], routed_rows(grads_ref), preferred_element_type=jnp.float32)
    store_shares(term * scale, mine_ref, theirs_ref)


def expert_in_grad_kernel(
    scale,
    slope_ref,
    out_weight_ref,
    rows_ref,
    grads_ref,
    mine_ref,
    theirs_ref,
    pre_grad_ref,
):
    hidden_grad = dot_rows(out_weight_ref[...], routed_rows(grads_ref))
    pre_grad = (hidden_grad * slope_ref[...]).astype(jnp.bfloat16)
    pre_grad_ref[...] = pre_grad
    term = jnp.dot(pre_grad, rows_ref[...], preferred_element_type=jnp.float32)
    store_shares(term * scale, mine_ref, theirs_ref)


def rows_back_kernel(pre_grad_ref, in_weight_ref, back_ref, total):
    step = pl.program_id(0)
    part = jnp.dot(in_weight_ref[...], pre_grad_ref[...], preferred_element_type=jnp.float32)

    @pl.when(step == 0)
    def _():
        total[...] = part

    @pl.when(step > 0)
    def _():
        total[...] += part

    @pl.when(step == pl.num_programs(0) - 1)
    def _():
        back_ref[...] = total[...].T.astype(back_ref.dtype)


def share_shapes(hidden, width):
    shape = (4, 2, hidden // 16, width)
    spec = pl.BlockSpec((1, *shape[1:]), lambda i: (i, 0, 0, 0))
    shapes = (
        jax.ShapeDtypeStruct(shape, jnp.float32),
        jax.ShapeDtypeStruct(shape, jnp.bfloat16),
    )
    return shapes, (spec, spec)


def expert_out_grad(hidden, grads, scale):
    units, count = hidden.shape
    width = grads.shape[2]
    shapes, specs = share_shapes(units, width)
    return pl.pallas_call(
        lambda *refs: expert_out_grad_kernel(scale, *refs),
        grid=(4,),
        out_shape=shapes,
        in_specs=[
            pl.BlockSpec((units // 4, count), lambda i: (i, 0)),
            pl.BlockSpec(grads.shape, lambda i: (0, 0, 0)),
        ],
        out_specs=specs,
        compiler_params=pltpu.CompilerParams(vmem_limit_bytes=EXPERT_VMEM),
        cost_estimate=pl.CostEstimate(
            flops=2 * units * count * width, transcendentals=0, bytes_accessed=2 * units * count
        ),
    )(hidden, grads)


def expert_in_grad(slopes, out_weight, rows, grads, scale):
    units, count = slopes.shape
    width = grads.shape[2]
    shapes, specs = share_shapes(units, width)
    return pl.pallas_call(
        lambda *refs: expert_in_grad_kernel(scale, *refs),
        grid=(4,),
        out_shape=(*shapes, jax.ShapeDtypeStruct((units, count), jnp.bfloat16)),
        in_specs=[
            pl.BlockSpec((units // 4, count), lambda i: (i, 0)),
            pl.BlockSpec((units // 4, width), lambda i: (i, 0)),
            pl.BlockSpec((count, width), lambda i: (0, 0)),
            pl.BlockSpec(grads.shape, lambda i: (0, 0, 0)),
        ],
        out_specs=(*specs, pl.BlockSpec((units // 4, count), lambda i: (i, 0))),
        compiler_params=pltpu.CompilerParams(vmem_limit_bytes=EXPERT_VMEM),
        cost_estimate=pl.CostEstimate(
            flops=4 * units * count * width, transcendentals=0, bytes_accessed=6 * units * count
        ),
    )(slopes, out_weight, rows, grads)


def rows_back(pre_grad, in_weight):
    units, count = pre_grad.shape
    width = in_weight.shape[0]
    return pl.pallas_call(
        rows_back_kernel,
        grid=(4,),
        out_shape=jax.ShapeDtypeStruct((count, width), jnp.bfloat16),
        in_specs=[
            pl.BlockSpec((units // 4, count), lambda i: (i, 0)),
            pl.BlockSpec((width, units // 4), lambda i: (0, i)),
        ],
        out_specs=pl.BlockSpec((count, width), lambda i: (0, 0)),
        scratch_shapes=[pltpu.VMEM((width, count), jnp.float32)],
        compiler_params=pltpu.CompilerParams(vmem_limit_bytes=EXPERT_VMEM),
        cost_estimate=pl.CostEstimate(
            flops=units * count, transcendentals=0, bytes_accessed=count * width
        ),
    )(pre_grad, in_weight)


def swap(block, distance):
    return hop(block.astype(jnp.bfloat16), "blk", lambda i: i ^ distance)


def swap_over_z(blocks):
    return [swap(blocks[d], 4 * d) for d in (1, 2, 3)]


def add_swapped(own, swapped):
    first, second, third = [block.astype(jnp.float32) for block in swapped]
    return own + (first + (second + third))


def local(
    nodes,
    attention_weights,
    output_weight,
    router_weight,
    gain_first,
    gain_second,
    expert_in,
    expert_out,
    routes,
    cotangent,
):
    exp_count = lax.axis_size("exp")
    blk_count = lax.axis_size("blk")
    block_rows = nodes.shape[0]
    width = nodes.shape[1]
    features = attention_weights.shape[1]
    own_rows = block_rows // exp_count
    capacity = 4 * block_rows // (exp_count * exp_count)
    experts = router_weight.shape[0]
    grad_scale = 1.0 / math.sqrt(block_rows * blk_count)
    projected = jnp.einsum(
        "fd,td->ft",
        attention_weights.reshape(3 * features, width),
        nodes,
        preferred_element_type=jnp.float32,
    ).astype(jnp.bfloat16)
    attended, lane_parts = attention(
        projected, output_weight, jnp.concatenate([expert_in, expert_out], axis=0), exp_count
    )
    flat_routes = routes.reshape(2 * own_rows)
    choose = (flat_routes[:, None] == jnp.arange(experts, dtype=jnp.int32)[None, :]).astype(
        jnp.int32
    )
    before = jnp.cumsum(choose, axis=0) - choose
    slot_index = jnp.sum(before * choose, axis=1)
    position = flat_routes * capacity + slot_index
    from_heads = exchange(attended)
    lane = jnp.stack(lane_parts)
    from_heads, lane, position = lax.optimization_barrier((from_heads, lane, position))
    attn_out = jnp.einsum(
        "hfr,hfd->rd",
        from_heads[:, :, width:],
        from_heads[:, :, :width],
        preferred_element_type=jnp.float32,
    )
    own_nodes = lax.dynamic_slice_in_dim(
        nodes, lax.axis_index("exp") * own_rows, own_rows, 0
    ).astype(jnp.float32)
    stream = rms_gain(own_nodes + attn_out, gain_first).astype(jnp.bfloat16)
    lane_partner = hop(lane, "blk", lambda i: i ^ 1)
    logits = jnp.dot(stream, router_weight.T, preferred_element_type=jnp.float32)
    dispatch_table = (
        jnp.arange(experts * capacity, dtype=jnp.int32)[:, None] == position[None, :]
    ).astype(jnp.bfloat16)
    selected = choose.reshape(own_rows, 2, experts).astype(jnp.float32)

    def gate_values(values):
        picked = jnp.sum(jax.nn.sigmoid(values)[:, None, :] * selected, axis=-1)
        return picked / jnp.sum(picked, axis=-1, keepdims=True)

    gates, gate_back = jax.vjp(gate_values, logits)
    repeated = jnp.repeat(stream, 2, axis=0)
    outgoing = jnp.dot(dispatch_table, repeated, preferred_element_type=jnp.float32).astype(
        jnp.bfloat16
    )
    outgoing = outgoing.reshape(experts, capacity, width)
    arrived = exchange(outgoing).reshape(experts * capacity, width)
    result = expert_forward(arrived, lane, lane_partner)
    returned = exchange(result.reshape(experts, capacity, width))
    kept, result = lax.optimization_barrier((arrived, result))
    hidden, slopes, out_weight, in_weight = expert_slopes(kept, lane, lane_partner)
    returned, hidden, slopes = lax.optimization_barrier((returned, hidden, slopes))
    expert_rows = jnp.einsum(
        "ps,pd->sd",
        dispatch_table,
        returned.reshape(experts * capacity, width),
        preferred_element_type=jnp.float32,
    )
    expert_rows = expert_rows.reshape(own_rows, 2, width)
    mixture = gates[:, 0:1] * expert_rows[:, 0] + gates[:, 1:2] * expert_rows[:, 1]
    stream_two = stream.astype(jnp.float32) + mixture
    normed, norm_back = jax.vjp(rms_gain, stream_two, gain_second)
    layer_out = normed.astype(jnp.bfloat16)
    grad_two, gain_part = norm_back(cotangent.astype(jnp.float32))
    gate_grads = jnp.sum(expert_rows * grad_two[:, None, :], axis=-1)
    logit_grad = gate_back(gate_grads)[0]
    router_part = jnp.dot(
        logit_grad.T, stream.astype(jnp.float32), precision=lax.Precision.HIGHEST
    )
    small = jnp.concatenate([router_part, gain_part[None, :]], axis=0) * grad_scale
    sum_rows = jnp.pad(small, ((0, SUM_ROWS - small.shape[0]), (0, 0))).astype(jnp.bfloat16)
    assigned_grads = (
        (gates[..., None] * grad_two[:, None, :]).astype(jnp.bfloat16).reshape(2 * own_rows, width)
    )
    padded = capacity + SUM_ROWS
    place = jnp.arange(experts * padded, dtype=jnp.int32)[:, None]
    row_experts = jnp.concatenate([flat_routes, jnp.full((SUM_ROWS,), -1, jnp.int32)])
    row_slots = jnp.concatenate([slot_index, capacity + jnp.arange(SUM_ROWS, dtype=jnp.int32)])
    anywhere = jnp.logical_or(place // padded == row_experts[None, :], row_experts[None, :] < 0)
    spread = jnp.logical_and(anywhere, place % padded == row_slots[None, :])
    grad_outgoing = jnp.dot(
        spread.astype(jnp.bfloat16),
        jnp.concatenate([assigned_grads, sum_rows], axis=0),
        preferred_element_type=jnp.float32,
    ).astype(jnp.bfloat16)
    grad_arrived = exchange(grad_outgoing.reshape(experts, padded, width))
    out_mine, out_theirs = expert_out_grad(hidden, grad_arrived, grad_scale)
    out_mine, out_theirs, grad_arrived = lax.optimization_barrier(
        (out_mine, out_theirs, grad_arrived)
    )
    sum_rows = jnp.sum(grad_arrived[:, capacity:].astype(jnp.float32), axis=0)
    sum_rows = sum_rows.astype(jnp.bfloat16)
    sums_swapped = swap(sum_rows, 1)
    out_swapped = swap(out_theirs, 1)
    in_mine, in_theirs, pre_grad = expert_in_grad(
        slopes, out_weight, kept, grad_arrived, grad_scale
    )
    in_swapped = swap(in_theirs, 1)
    sums_swapped, out_swapped, in_mine, pre_grad = lax.optimization_barrier(
        (sums_swapped, out_swapped, in_mine, pre_grad)
    )
    sum_rows = (sum_rows.astype(jnp.float32) + sums_swapped.astype(jnp.float32)).astype(
        jnp.bfloat16
    )
    out_sums = out_mine + out_swapped.astype(jnp.float32)
    out_sent = add_rows(out_sums[:, 1].astype(jnp.bfloat16), sum_rows)
    out_beside = swap(out_sent, 2)
    out_sent, out_sums, pre_grad = lax.optimization_barrier((out_sent, out_sums, pre_grad))
    row_grads = rows_back(pre_grad, in_weight)
    in_mine, in_swapped, row_grads = lax.optimization_barrier((in_mine, in_swapped, row_grads))
    back_home = exchange(row_grads.reshape(experts, capacity, width))
    in_sums = in_mine + in_swapped.astype(jnp.float32)
    in_parts = swap_over_z(in_sums)
    out_beside, in_sums = lax.optimization_barrier((out_beside, in_sums))
    sum_rows = (
        out_sent[-SUM_ROWS:].astype(jnp.float32) + out_beside[-SUM_ROWS:].astype(jnp.float32)
    ).astype(jnp.bfloat16)
    out_sums = out_sums[:, 0] + out_beside[:-SUM_ROWS].reshape(out_sums.shape[:1] + out_sums.shape[2:])
    out_parts = [
        swap(add_rows(out_sums[d].astype(jnp.bfloat16), sum_rows), 4 * d) for d in (1, 2, 3)
    ]
    expert_out_grads = add_swapped(out_sums[0], [part[:-SUM_ROWS] for part in out_parts])[None]
    first, second, third = [part[-SUM_ROWS:].astype(jnp.float32) for part in out_parts]
    sums = (sum_rows.astype(jnp.float32) + first) + (second + third)
    router_grad, gain_grad = sums[:experts], sums[experts]
    in_sums = add_swapped(in_sums[0], in_parts)
    in_beside = swap(in_sums[1], 2)
    back_home, in_beside, expert_out_grads = lax.optimization_barrier(
        (back_home, in_beside, expert_out_grads)
    )
    expert_in_grads = (in_sums[0] + in_beside.astype(jnp.float32))[None]
    back_rows = jnp.einsum(
        "ps,pd->sd",
        dispatch_table,
        back_home.reshape(experts * capacity, width),
        preferred_element_type=jnp.float32,
    )
    back_rows = back_rows.reshape(own_rows, 2, width)
    router_term = jnp.dot(
        logit_grad, router_weight.astype(jnp.float32), precision=lax.Precision.HIGHEST
    )
    stream_grad = (grad_two + (back_rows[:, 0] + back_rows[:, 1]) + router_term).astype(
        jnp.bfloat16
    )
    return (layer_out, stream_grad, expert_in_grads, expert_out_grads, router_grad, gain_grad)


def solution(mesh):
    placed = (
        P("blk", None),
        P(None, "exp", None),
        P("exp", None),
        P(),
        P(),
        P(),
        P("exp", "blk", None),
        P("exp", "blk", None),
        P(("blk", "exp"), None),
        P(("blk", "exp"), None),
    )
    return jax.shard_map(
        local,
        mesh=mesh,
        in_specs=placed,
        out_specs=(
            P(("blk", "exp"), None),
            P(("blk", "exp"), None),
            P("exp", "blk", None),
            P("exp", "blk", None),
            P(),
            P(),
        ),
        check_vma=False,
    )
```

profile of v0, /device:TPU:0, one launch (start us, length us, event | category | flops | bytes accessed | tf_op | source)
XLA Modules:
  0.0 273.5 jit_solution(4022079155035900988)
XLA Ops:
  0.7 0.9 copy-done
  1.5 2.0 convolution_convert_fusion.refs_0_.refs_2_
  3.6 4.0 %collective-permute-start.4 = (bf16[64,1536]{1,0:T(8,128)(2,1)S(1)}, bf16[64,1536]{1,0:T(8,128)(2,1)S(1)}, u32[]{:S(2)}, u32[]{:S(2)}) collective-permute-start(bf16[64,1536]{1,0:T(8,128)(2,1)S(1)} %slice.148), channel_id=1, source_target_pairs={{0,64},{8,72},{16,80},{24,88},{32,96},{40,104},{48,112},{56,120},{... | collective-permute-start | bytes 589832 | tf_op jit(solution)/shard_map/ppermute | solution.py:33
  7.6 0.7 collective-permute-start.3
  8.6 1.6 collective-permute-start.1
  10.6 0.9 reduce-window.6
  11.9 5.0 %shard_map.145 = (bf16[128,1536]{1,0:T(8,128)(2,1)S(1)}, f32[48,1536]{1,0:T(8,128)S(1)}) custom-call(bf16[96,1536]{1,0:T(8,128)(2,1)S(1)} %convolution_convert_fusion.refs_0_.refs_2_, bf16[64,1536]{1,0:T(8,128)(2,1)S(1)} %collective-permute-done.refs_1_.refs_5_), custom_call_target="tpu_custom_call" | custom-call | flops 5662310400 | bytes 393216 | tf_op jit(solution)/shard_map/pallas_call | solution.py:153
  17.6 1.7 collective-permute-start.5
  19.4 9.7 %shard_map.146.refs_1_ = f32[48,1536]{1,0:T(8,128)S(1)} custom-call(bf16[128,1536]{1,0:T(8,128)(2,1)S(1)} %get-tuple-element.55.refs_0_, f32[48,1536]{1,0:T(8,128)S(1)} %get-tuple-element.61.refs_1_, bf16[64,1536]{1,0:T(8,128)(2,1)S(1)} %collective-permute-done.1.refs_2_.refs_6_, ...), custom_call_target="tpu_custom_call", output_to_operand_aliasing={{}: (1, {})} | custom-call | flops 11324620800 | bytes 786432 | tf_op jit(solution)/shard_map/pallas_call | solution.py:153
  29.6 9.8 %shard_map.147.refs_1_ = f32[48,1536]{1,0:T(8,128)S(1)} custom-call(bf16[128,1536]{1,0:T(8,128)(2,1)S(1)} %get-tuple-element.55.refs_0_, f32[48,1536]{1,0:T(8,128)S(1)} %shard_map.146.refs_1_, bf16[256,1536]{1,0:T(8,128)(2,1)S(1)} %collective-permute-done.6.refs_2_.refs_10_), custom_call_target="tpu_custom_call", output_to_operand_aliasing={{}: (1, {})} | custom-call | flops 11324620800 | bytes 786432 | tf_op jit(solution)/shard_map/pallas_call | solution.py:153
  39.5 3.5 %collective-permute-start.10 = (bf16[2,2,128,512]{3,2,1,0:T(8,128)(2,1)S(1)}, bf16[2,2,128,512]{3,2,1,0:T(8,128)(2,1)S(1)}, u32[]{:S(2)}, u32[]{:S(2)}) collective-permute-start(bf16[2,2,128,512]{3,2,1,0:T(8,128)(2,1)S(1)} %get-tuple-element.121), channel_id=1, source_target_pairs={{0,64},{8,72},{16,80},{24,88},{32,96},{40,104},{48,112},{56,120},{... | collective-permute-start | bytes 1572872 | tf_op jit(solution)/shard_map/ppermute | solution.py:33
  43.1 0.6 collective-permute-start.11
  43.7 7.3 %shard_map.148.refs_1_ = f32[48,1536]{1,0:T(8,128)S(1)} custom-call(bf16[128,1536]{1,0:T(8,128)(2,1)S(1)} %get-tuple-element.55.refs_0_, f32[48,1536]{1,0:T(8,128)S(1)} %shard_map.147.refs_1_, bf16[192,1536]{1,0:T(8,128)(2,1)S(1)} %collective-permute-done.5.refs_2_.refs_11_), custom_call_target="tpu_custom_call", output_to_operand_aliasing={{}: (1, {})} | custom-call | flops 8493465600 | bytes 589824 | tf_op jit(solution)/shard_map/pallas_call | solution.py:153
  51.1 75.7 %shard_map.149 = bf16[8,32,704]{2,1,0:T(8,128)(2,1)} custom-call(bf16[128,1536]{1,0:T(8,128)(2,1)S(1)} %get-tuple-element.55.refs_0_, f32[48,1536]{1,0:T(8,128)S(1)} %shard_map.148.refs_1_, bf16[96,1536]{1,0:T(8,128)(2,1)S(1)} %convolution_convert_fusion.refs_0_.refs_2_, bf16[32,512]{1,0:T(8,128)(2,1)S(1)} %copy-done.10, ...), custom_call_target="tpu_custom_call" | custom-call | flops 8493465600 | bytes 589824 | tf_op jit(solution)/shard_map/pallas_call | solution.py:153
  126.8 6.9 %all-to-all-start = ((bf16[8,32,704]{2,1,0:T(8,128)(2,1)}), bf16[8,32,704]{2,1,0:T(8,128)(2,1)S(1)}, u32[]{:S(2)}, u32[]{:S(2)}) async-start(bf16[8,32,704]{2,1,0:T(8,128)(2,1)} %shard_map.149), calls=%async_computation | async-start | bytes 786432 | tf_op jit(solution)/shard_map/all_to_all | solution.py:28
  133.8 0.8 copy-done.19
  134.8 1.6 pad_maximum_fusion.in_lane.out_lane
  136.4 8.2 %all-to-all-done = bf16[8,32,704]{2,1,0:T(8,128)(2,1)S(1)} async-done(((bf16[8,32,704]{2,1,0:T(8,128)(2,1)}), bf16[8,32,704]{2,1,0:T(8,128)(2,1)S(1)}, u32[]{:S(2)}, u32[]{:S(2)}) %all-to-all-start) | async-done | bytes 360480 | tf_op jit(solution)/shard_map/all_to_all | solution.py:28
  144.6 1.3 multiply_reduce_fusion.2
  145.9 0.8 copy-done.15
  147.1 1.5 convolution_convert_fusion.1
  148.6 3.5 %all-to-all-start.1 = ((bf16[8,96,512]{2,1,0:T(8,128)(2,1)}), bf16[8,96,512]{2,1,0:T(8,128)(2,1)S(1)}, u32[]{:S(2)}, u32[]{:S(2)}) async-start(bf16[8,96,512]{2,1,0:T(8,128)(2,1)} %bitcast.116), calls=%async_computation.1 | async-start | bytes 1572864 | tf_op jit(solution)/shard_map/all_to_all | solution.py:28
  152.7 14.8 %all-to-all-done.1 = bf16[8,96,512]{2,1,0:T(8,128)(2,1)S(1)} async-done(((bf16[8,96,512]{2,1,0:T(8,128)(2,1)}), bf16[8,96,512]{2,1,0:T(8,128)(2,1)S(1)}, u32[]{:S(2)}, u32[]{:S(2)}) %all-to-all-start.1) | async-done | bytes 786464 | tf_op jit(solution)/shard_map/all_to_all | solution.py:28
  167.5 6.7 %shard_map.150 = bf16[768,512]{1,0:T(8,128)(2,1)S(1)} custom-call(bf16[768,512]{1,0:T(8,128)(2,1)S(1)} %bitcast.106, bf16[4,2,2,128,512]{4,3,2,1,0:T(8,128)(2,1)S(1)} %pad_maximum_fusion.in_lane.out_lane, bf16[4,2,2,128,512]{4,3,2,1,0:T(8,128)(2,1)} %collective-permute-done.12.in_partner.out_partner, ...), custom_call_target="tpu_custom_call" | custom-call | flops 3221225472 | bytes 4194304 | tf_op jit(solution)/shard_map/pallas_call | solution.py:285
  174.2 0.9 copy-done.4
  175.1 4.4 %all-to-all-start.2 = ((bf16[8,96,512]{2,1,0:T(8,128)(2,1)}), bf16[8,96,512]{2,1,0:T(8,128)(2,1)}, u32[]{:S(2)}, u32[]{:S(2)}) async-start(bf16[8,96,512]{2,1,0:T(8,128)(2,1)} %bitcast.109), calls=%async_computation.2 | async-start | bytes 1572864 | tf_op jit(solution)/shard_map/all_to_all | solution.py:28
  179.8 1.1 eq.102
  180.9 6.6 %shard_map.151 = (bf16[2048,768]{1,0:T(8,128)(2,1)S(1)}, f32[2048,768]{1,0:T(8,128)S(1)}, bf16[2048,512]{1,0:T(8,128)(2,1)S(1)}, bf16[512,2048]{1,0:T(8,128)(2,1)S(1)}) custom-call(bf16[768,512]{1,0:T(8,128)(2,1)S(1)} %bitcast.107, bf16[4,2,2,128,512]{4,3,2,1,0:T(8,128)(2,1)S(1)} %pad_maximum_fusion.in_lane.out_lane, ...), custom_call_target="tpu_custom_call" | custom-call | flops 1610612736 | bytes 17825792 | tf_op jit(solution)/shard_map/pallas_call | solution.py:328
  187.6 1.3 copy-done.2
  188.9 2.6 copy-done.5
  191.5 1.7 copy-done.6
  193.2 1.4 copy-done.8
  194.6 1.8 fusion.37
  197.0 0.8 add_add_fusion
  198.5 0.5 mul.202
  199.2 0.8 fusion.5
  200.0 22.4 %all_to_all.25.refs_1_.refs_3_ = bf16[8,112,512]{2,1,0:T(8,128)(2,1)S(1)} all-to-all(bf16[8,112,512]{2,1,0:T(8,128)(2,1)S(1)} %bitcast.115), channel_id=1, replica_groups=mesh['blk'=16,'exp'=8] {'exp'}, dimensions={0} | all-to-all | bytes 1835008 | tf_op jit(solution)/shard_map/all_to_all | solution.py:28
  222.4 2.3 shard_map.152
  224.9 4.1 %shard_map.153 = (f32[4,2,128,512]{3,2,1,0:T(8,128)S(1)}, bf16[4,2,128,512]{3,2,1,0:T(8,128)(2,1)S(1)}, bf16[2048,768]{1,0:T(8,128)(2,1)S(1)}) custom-call(f32[2048,768]{1,0:T(8,128)S(1)} %bitcast.111, bf16[2048,512]{1,0:T(8,128)(2,1)S(1)} %copy-done.9, bf16[768,512]{1,0:T(8,128)(2,1)S(1)} %bitcast.108, bf16[8,112,512]{2,1,0:T(8,128)(2,1)S(1)} %all_to_all.25.refs_1_.refs_3_), custom_call_target="tpu_custom_call" | custom-call | flops 3221225472 | bytes 9437184 | tf_op jit(solution)/shard_map/pallas_call | solution.py:439
  229.0 0.6 collective-permute-start.15
  229.7 2.1 collective-permute-done.13
  232.1 1.4 copy-done.11
  233.6 0.7 collective-permute-start.16
  234.4 0.7 copy-done.3
  235.1 4.2 %shard_map.154 = bf16[768,512]{1,0:T(8,128)(2,1)} custom-call(bf16[2048,768]{1,0:T(8,128)(2,1)S(1)} %get-tuple-element.92.pre_grad_ref, bf16[512,2048]{1,0:T(8,128)(2,1)S(1)} %copy-done.3), custom_call_target="tpu_custom_call" | custom-call | flops 1572864 | bytes 393216 | tf_op jit(solution)/shard_map/pallas_call | solution.py:460
  239.2 4.2 %all-to-all-start.4 = ((bf16[8,96,512]{2,1,0:T(8,128)(2,1)}), bf16[8,96,512]{2,1,0:T(8,128)(2,1)}, u32[]{:S(2)}, u32[]{:S(2)}) async-start(bf16[8,96,512]{2,1,0:T(8,128)(2,1)} %bitcast.22), calls=%async_computation.4 | async-start | bytes 1572864 | tf_op jit(solution)/shard_map/all_to_all | solution.py:28
  243.5 1.6 fusion.72
  245.2 1.2 collective-permute-start.17
  246.4 2.5 collective-permute-start.19
  249.5 1.1 slice.130
  250.8 0.7 add_convert_fusion
  251.6 4.9 %collective-permute-start.21 = (bf16[144,512]{1,0:T(8,128)(2,1)S(1)}, bf16[144,512]{1,0:T(8,128)(2,1)S(1)}, u32[]{:S(2)}, u32[]{:S(2)}) collective-permute-start(bf16[144,512]{1,0:T(8,128)(2,1)S(1)} %get-tuple-element.124), channel_id=1, source_target_pairs={{0,32},{8,40},{16,48},{24,56},{32,0},{40,8},{48,16},{56,24},{64,96... | collective-permute-start | bytes 442376 | tf_op jit(solution)/shard_map/ppermute | solution.py:33
  256.5 2.1 collective-permute-start.22
  258.6 0.7 collective-permute-start.23
  259.3 2.1 collective-permute-done.19
  261.3 0.8 collective-permute-done.18
  262.3 0.7 collective-permute-start.20
  263.2 4.8 %collective-permute-done.22 = bf16[144,512]{1,0:T(8,128)(2,1)S(1)} collective-permute-done((bf16[144,512]{1,0:T(8,128)(2,1)S(1)}, bf16[144,512]{1,0:T(8,128)(2,1)S(1)}, u32[]{:S(2)}, u32[]{:S(2)}) %collective-permute-start.22) | collective-permute-done | bytes 147488 | tf_op jit(solution)/shard_map/ppermute | solution.py:33
  268.1 0.6 slice.173
  268.7 0.6 slice.172
  269.3 0.8 fusion.42
  270.1 0.7 fusion.40
  270.8 1.6 fusion.35
  272.4 1.1 fusion.9
  (136 shorter events, 7.3 us)
Async XLA Ops:
  0.6 0.9 copy-start
  0.6 9.6 %copy-start.24 = (s32[192,2]{0,1:T(2,128)S(1)}, s32[192,2]{0,1:T(2,128)}, u32[]{:S(2)}) copy-start(s32[192,2]{0,1:T(2,128)} %param.18) | copy-start | bytes 4612
  0.7 11.2 %copy-start.21 = (bf16[1,128,512]{2,1,0:T(8,128)(2,1)S(1)}, bf16[1,128,512]{2,1,0:T(8,128)(2,1)}, u32[]{:S(2)}) copy-start(bf16[1,128,512]{2,1,0:T(8,128)(2,1)} %param.17) | copy-start | bytes 393220
  0.7 11.2 %copy-start.22 = (bf16[1,128,512]{2,1,0:T(8,128)(2,1)S(1)}, bf16[1,128,512]{2,1,0:T(8,128)(2,1)}, u32[]{:S(2)}) copy-start(bf16[1,128,512]{2,1,0:T(8,128)(2,1)} %param.16) | copy-start | bytes 393220
  3.6 13.4 %collective-permute-start.4 = (bf16[64,1536]{1,0:T(8,128)(2,1)S(1)}, bf16[64,1536]{1,0:T(8,128)(2,1)S(1)}, u32[]{:S(2)}, u32[]{:S(2)}) collective-permute-start(bf16[64,1536]{1,0:T(8,128)(2,1)S(1)} %slice.148), channel_id=1, source_target_pairs={{0,64},{8,72},{16,80},{24,88},{32,96},{40,104},{48,112},{56,120},{... | collective-permute-start | bytes 589832 | tf_op jit(solution)/shard_map/ppermute | solution.py:33
  7.6 9.4 %collective-permute-start.3 = (bf16[64,1536]{1,0:T(8,128)(2,1)S(1)}, bf16[64,1536]{1,0:T(8,128)(2,1)S(1)}, u32[]{:S(2)}, u32[]{:S(2)}) collective-permute-start(bf16[64,1536]{1,0:T(8,128)(2,1)S(1)} %slice.148), channel_id=1, source_target_pairs={{0,96},{8,104},{16,112},{24,120},{32,64},{40,72},{48,80},{56,88},{... | collective-permute-start | bytes 589832 | tf_op jit(solution)/shard_map/ppermute | solution.py:33
  8.3 9.2 %collective-permute-start.2 = (bf16[64,1536]{1,0:T(8,128)(2,1)S(1)}, bf16[64,1536]{1,0:T(8,128)(2,1)S(1)}, u32[]{:S(2)}, u32[]{:S(2)}) collective-permute-start(bf16[64,1536]{1,0:T(8,128)(2,1)S(1)} %slice.148), channel_id=1, source_target_pairs={{0,32},{8,40},{16,48},{24,56},{32,0},{40,8},{48,16},{56,24},{64,96... | collective-permute-start | bytes 589832 | tf_op jit(solution)/shard_map/ppermute | solution.py:33
  8.6 8.9 %collective-permute-start.1 = (bf16[64,1536]{1,0:T(8,128)(2,1)S(1)}, bf16[64,1536]{1,0:T(8,128)(2,1)S(1)}, u32[]{:S(2)}, u32[]{:S(2)}) collective-permute-start(bf16[64,1536]{1,0:T(8,128)(2,1)S(1)} %slice.148), channel_id=1, source_target_pairs={{0,16},{8,24},{16,0},{24,8},{32,48},{40,56},{48,32},{56,40},{64,80... | collective-permute-start | bytes 589832 | tf_op jit(solution)/shard_map/ppermute | solution.py:33
  10.2 1.7 collective-permute-start
  17.6 21.9 %collective-permute-start.5 = (bf16[192,1536]{1,0:T(8,128)(2,1)S(1)}, bf16[192,1536]{1,0:T(8,128)(2,1)S(1)}, u32[]{:S(2)}, u32[]{:S(2)}) collective-permute-start(bf16[192,1536]{1,0:T(8,128)(2,1)S(1)} %pad_maximum_fusion.2), channel_id=1, source_target_pairs={{0,16},{8,24},{16,0},{24,8},{32,48},{40,56},{48,32},{56,40},{64,80... | collective-permute-start | bytes 1769480 | tf_op jit(solution)/shard_map/ppermute | solution.py:33
  19.3 9.9 %collective-permute-start.6 = (bf16[256,1536]{1,0:T(8,128)(2,1)S(1)}, bf16[256,1536]{1,0:T(8,128)(2,1)S(1)}, u32[]{:S(2)}, u32[]{:S(2)}) collective-permute-start(bf16[256,1536]{1,0:T(8,128)(2,1)S(1)} %pad_maximum_fusion.1), channel_id=1, source_target_pairs={{0,8},{8,0},{16,24},{24,16},{32,40},{40,32},{48,56},{56,48},{64,72... | collective-permute-start | bytes 2359304 | tf_op jit(solution)/shard_map/ppermute | solution.py:33
  29.1 10.3 %collective-permute-start.7 = (bf16[2,128,512]{2,1,0:T(8,128)(2,1)S(1)}, bf16[2,128,512]{2,1,0:T(8,128)(2,1)S(1)}, u32[]{:S(2)}, u32[]{:S(2)}) collective-permute-start(bf16[2,128,512]{2,1,0:T(8,128)(2,1)S(1)} %pad_maximum_fusion.5), channel_id=1, source_target_pairs={{0,16},{8,24},{16,0},{24,8},{32,48},{40,56},{48,32},{56,40},{64,80... | collective-permute-start | bytes 786440 | tf_op jit(solution)/shard_map/ppermute | solution.py:33
  39.5 11.6 %copy-start.10 = (bf16[32,512]{1,0:T(8,128)(2,1)S(1)}, bf16[32,512]{1,0:T(8,128)(2,1)}, u32[]{:S(2)}) copy-start(bf16[32,512]{1,0:T(8,128)(2,1)} %refs_3_.1) | copy-start | bytes 98308
  39.5 94.2 %collective-permute-start.10 = (bf16[2,2,128,512]{3,2,1,0:T(8,128)(2,1)S(1)}, bf16[2,2,128,512]{3,2,1,0:T(8,128)(2,1)S(1)}, u32[]{:S(2)}, u32[]{:S(2)}) collective-permute-start(bf16[2,2,128,512]{3,2,1,0:T(8,128)(2,1)S(1)} %get-tuple-element.121), channel_id=1, source_target_pairs={{0,64},{8,72},{16,80},{24,88},{32,96},{40,104},{48,112},{56,120},{... | collective-permute-start | bytes 1572872 | tf_op jit(solution)/shard_map/ppermute | solution.py:33
  43.0 90.8 %collective-permute-start.9 = (bf16[2,2,128,512]{3,2,1,0:T(8,128)(2,1)S(1)}, bf16[2,2,128,512]{3,2,1,0:T(8,128)(2,1)S(1)}, u32[]{:S(2)}, u32[]{:S(2)}) collective-permute-start(bf16[2,2,128,512]{3,2,1,0:T(8,128)(2,1)S(1)} %get-tuple-element.121), channel_id=1, source_target_pairs={{0,32},{8,40},{16,48},{24,56},{32,0},{40,8},{48,16},{56,24},{64,96... | collective-permute-start | bytes 1572872 | tf_op jit(solution)/shard_map/ppermute | solution.py:33
  43.1 90.7 %collective-permute-start.11 = (bf16[2,2,128,512]{3,2,1,0:T(8,128)(2,1)S(1)}, bf16[2,2,128,512]{3,2,1,0:T(8,128)(2,1)}, u32[]{:S(2)}, u32[]{:S(2)}) collective-permute-start(bf16[2,2,128,512]{3,2,1,0:T(8,128)(2,1)S(1)} %get-tuple-element.121), channel_id=1, source_target_pairs={{0,96},{8,104},{16,112},{24,120},{32,64},{40,72},{48,80},{56,88},{... | collective-permute-start | bytes 1572872 | tf_op jit(solution)/shard_map/ppermute | solution.py:33
  43.7 7.4 %collective-permute-start.8 = (bf16[192,1536]{1,0:T(8,128)(2,1)S(1)}, bf16[192,1536]{1,0:T(8,128)(2,1)S(1)}, u32[]{:S(2)}, u32[]{:S(2)}) collective-permute-start(bf16[192,1536]{1,0:T(8,128)(2,1)S(1)} %collective-permute-done.5.refs_2_.refs_11_), channel_id=1, source_target_pairs={{0,8},{8,0},{16,24},{24,16},{32,40},{40,32},{48,56},{56,48},{64,72... | collective-permute-start | bytes 1769480 | tf_op jit(solution)/shard_map/ppermute | solution.py:33
  126.8 17.8 %all-to-all-start = ((bf16[8,32,704]{2,1,0:T(8,128)(2,1)}), bf16[8,32,704]{2,1,0:T(8,128)(2,1)S(1)}, u32[]{:S(2)}, u32[]{:S(2)}) async-start(bf16[8,32,704]{2,1,0:T(8,128)(2,1)} %shard_map.149), calls=%async_computation | async-start | bytes 786432 | tf_op jit(solution)/shard_map/all_to_all | solution.py:28
  133.7 0.8 copy-start.19
  133.8 1.0 copy-start.20
  134.8 11.9 %copy-start.25 = (f32[512]{0:T(512)S(1)}, f32[512]{0:T(512)}, u32[]{:S(2)}) copy-start(f32[512]{0:T(512)} %param.14) | copy-start | bytes 6148
  144.6 22.9 %collective-permute-start.12 = (bf16[4,2,2,128,512]{4,3,2,1,0:T(8,128)(2,1)S(1)}, bf16[4,2,2,128,512]{4,3,2,1,0:T(8,128)(2,1)}, u32[]{:S(2)}, u32[]{:S(2)}) collective-permute-start(bf16[4,2,2,128,512]{4,3,2,1,0:T(8,128)(2,1)S(1)} %pad_maximum_fusion.in_lane.out_lane), channel_id=1, source_target_pairs={{0,8},{8,0},{16,24},{24,16},{32,40},{40,32},{48,56},{56,48},{64,72... | collective-permute-start | bytes 6291464 | tf_op jit(solution)/shard_map/ppermute | solution.py:33
  145.9 0.8 copy-start.15
  146.8 5.5 %copy-start.13 = (bf16[192,512]{1,0:T(8,128)(2,1)}, bf16[192,512]{1,0:T(8,128)(2,1)S(1)}, u32[]{:S(2)}) copy-start(bf16[192,512]{1,0:T(8,128)(2,1)S(1)} %multiply_convert_fusion.2) | copy-start | bytes 589828
  147.0 5.3 %copy-start.23 = (bf16[8,512]{1,0:T(8,128)(2,1)S(1)}, bf16[8,512]{1,0:T(8,128)(2,1)}, u32[]{:S(2)}) copy-start(bf16[8,512]{1,0:T(8,128)(2,1)} %param.13) | copy-start | bytes 24580
  148.6 18.8 %all-to-all-start.1 = ((bf16[8,96,512]{2,1,0:T(8,128)(2,1)}), bf16[8,96,512]{2,1,0:T(8,128)(2,1)S(1)}, u32[]{:S(2)}, u32[]{:S(2)}) async-start(bf16[8,96,512]{2,1,0:T(8,128)(2,1)} %bitcast.116), calls=%async_computation.1 | async-start | bytes 1572864 | tf_op jit(solution)/shard_map/all_to_all | solution.py:28
  174.2 0.9 copy-start.4
  175.1 19.5 %all-to-all-start.2 = ((bf16[8,96,512]{2,1,0:T(8,128)(2,1)}), bf16[8,96,512]{2,1,0:T(8,128)(2,1)}, u32[]{:S(2)}, u32[]{:S(2)}) async-start(bf16[8,96,512]{2,1,0:T(8,128)(2,1)} %bitcast.109), calls=%async_computation.2 | async-start | bytes 1572864 | tf_op jit(solution)/shard_map/all_to_all | solution.py:28
  187.5 1.3 copy-start.2
  188.9 2.6 copy-start.5
  191.5 1.7 copy-start.6
  193.2 1.4 copy-start.8
  194.6 1.9 copy-start.16
  194.6 2.2 copy-start.17
  194.6 2.2 copy-start.26
  196.7 1.3 copy-start.14
  199.1 23.4 %copy-start.7 = (bf16[2048,768]{1,0:T(8,128)(2,1)S(1)}, bf16[2048,768]{1,0:T(8,128)(2,1)}, u32[]{:S(2)}) copy-start(bf16[2048,768]{1,0:T(8,128)(2,1)} %copy-done.6) | copy-start | bytes 9437188
  199.2 25.6 %slice-start = ((s8[6291456]{0:T(1024)(128)(4,1)}), s8[4194304]{0:T(1024)(128)(4,1)S(1)}, s32[]{:S(2)}) async-start(s8[6291456]{0:T(1024)(128)(4,1)} %bitcast.110), calls=%async_computation.5 | async-start | bytes 8388608
  200.0 24.9 %slice-start.1 = ((s8[6291456]{0:T(1024)(128)(4,1)}), s8[2097152]{0:T(1024)(128)(4,1)S(1)}, s32[]{:S(2)}) async-start(s8[6291456]{0:T(1024)(128)(4,1)} %bitcast.110), calls=%async_computation.6 | async-start | bytes 4194304
  222.4 2.4 copy-start.9
  224.8 7.0 %collective-permute-start.14 = (bf16[4,2,128,512]{3,2,1,0:T(8,128)(2,1)S(1)}, bf16[4,2,128,512]{3,2,1,0:T(8,128)(2,1)S(1)}, u32[]{:S(2)}, u32[]{:S(2)}) collective-permute-start(bf16[4,2,128,512]{3,2,1,0:T(8,128)(2,1)S(1)} %get-tuple-element.81), channel_id=1, source_target_pairs={{0,8},{8,0},{16,24},{24,16},{32,40},{40,32},{48,56},{56,48},{64,72... | collective-permute-start | bytes 3145736 | tf_op jit(solution)/shard_map/ppermute | solution.py:33
  229.0 10.2 %collective-permute-start.15 = (bf16[4,2,128,512]{3,2,1,0:T(8,128)(2,1)S(1)}, bf16[4,2,128,512]{3,2,1,0:T(8,128)(2,1)}, u32[]{:S(2)}, u32[]{:S(2)}) collective-permute-start(bf16[4,2,128,512]{3,2,1,0:T(8,128)(2,1)S(1)} %get-tuple-element.87), channel_id=1, source_target_pairs={{0,8},{8,0},{16,24},{24,16},{32,40},{40,32},{48,56},{56,48},{64,72... | collective-permute-start | bytes 3145736 | tf_op jit(solution)/shard_map/ppermute | solution.py:33
  229.6 2.2 collective-permute-start.13
  232.1 1.4 copy-start.11
  233.5 1.6 copy-start.3
  233.6 15.9 %collective-permute-start.16 = (bf16[528,512]{1,0:T(8,128)(2,1)S(1)}, bf16[528,512]{1,0:T(8,128)(2,1)}, u32[]{:S(2)}, u32[]{:S(2)}) collective-permute-start(bf16[528,512]{1,0:T(8,128)(2,1)S(1)} %pad_maximum_fusion.3), channel_id=1, source_target_pairs={{0,16},{8,24},{16,0},{24,8},{32,48},{40,56},{48,32},{56,40},{64,80... | collective-permute-start | bytes 1622024 | tf_op jit(solution)/shard_map/ppermute | solution.py:33
  239.2 30.8 %all-to-all-start.4 = ((bf16[8,96,512]{2,1,0:T(8,128)(2,1)}), bf16[8,96,512]{2,1,0:T(8,128)(2,1)}, u32[]{:S(2)}, u32[]{:S(2)}) async-start(bf16[8,96,512]{2,1,0:T(8,128)(2,1)} %bitcast.22), calls=%async_computation.4 | async-start | bytes 1572864 | tf_op jit(solution)/shard_map/all_to_all | solution.py:28
  245.1 5.5 %copy-start.12 = (f32[4,2,128,512]{3,2,1,0:T(8,128)S(1)}, f32[4,2,128,512]{3,2,1,0:T(8,128)}, u32[]{:S(2)}) copy-start(f32[4,2,128,512]{3,2,1,0:T(8,128)} %copy-done.11) | copy-start | bytes 6291460
  245.2 13.4 %collective-permute-start.17 = (bf16[2,128,512]{2,1,0:T(8,128)(2,1)S(1)}, bf16[2,128,512]{2,1,0:T(8,128)(2,1)S(1)}, u32[]{:S(2)}, u32[]{:S(2)}) collective-permute-start(bf16[2,128,512]{2,1,0:T(8,128)(2,1)S(1)} %get-tuple-element.114), channel_id=1, source_target_pairs={{0,32},{8,40},{16,48},{24,56},{32,0},{40,8},{48,16},{56,24},{64,96... | collective-permute-start | bytes 786440 | tf_op jit(solution)/shard_map/ppermute | solution.py:33
  246.4 14.9 %collective-permute-start.19 = (bf16[2,128,512]{2,1,0:T(8,128)(2,1)S(1)}, bf16[2,128,512]{2,1,0:T(8,128)(2,1)S(1)}, u32[]{:S(2)}, u32[]{:S(2)}) collective-permute-start(bf16[2,128,512]{2,1,0:T(8,128)(2,1)S(1)} %get-tuple-element.115), channel_id=1, source_target_pairs={{0,96},{8,104},{16,112},{24,120},{32,64},{40,72},{48,80},{56,88},{... | collective-permute-start | bytes 786440 | tf_op jit(solution)/shard_map/ppermute | solution.py:33
  249.0 13.1 %collective-permute-start.18 = (bf16[2,128,512]{2,1,0:T(8,128)(2,1)S(1)}, bf16[2,128,512]{2,1,0:T(8,128)(2,1)S(1)}, u32[]{:S(2)}, u32[]{:S(2)}) collective-permute-start(bf16[2,128,512]{2,1,0:T(8,128)(2,1)S(1)} %get-tuple-element.116), channel_id=1, source_target_pairs={{0,64},{8,72},{16,80},{24,88},{32,96},{40,104},{48,112},{56,120},{... | collective-permute-start | bytes 786440 | tf_op jit(solution)/shard_map/ppermute | solution.py:33
  251.6 11.6 %collective-permute-start.21 = (bf16[144,512]{1,0:T(8,128)(2,1)S(1)}, bf16[144,512]{1,0:T(8,128)(2,1)S(1)}, u32[]{:S(2)}, u32[]{:S(2)}) collective-permute-start(bf16[144,512]{1,0:T(8,128)(2,1)S(1)} %get-tuple-element.124), channel_id=1, source_target_pairs={{0,32},{8,40},{16,48},{24,56},{32,0},{40,8},{48,16},{56,24},{64,96... | collective-permute-start | bytes 442376 | tf_op jit(solution)/shard_map/ppermute | solution.py:33
  256.5 11.5 %collective-permute-start.22 = (bf16[144,512]{1,0:T(8,128)(2,1)S(1)}, bf16[144,512]{1,0:T(8,128)(2,1)S(1)}, u32[]{:S(2)}, u32[]{:S(2)}) collective-permute-start(bf16[144,512]{1,0:T(8,128)(2,1)S(1)} %get-tuple-element.125), channel_id=1, source_target_pairs={{0,64},{8,72},{16,80},{24,88},{32,96},{40,104},{48,112},{56,120},{... | collective-permute-start | bytes 442376 | tf_op jit(solution)/shard_map/ppermute | solution.py:33
  258.6 12.2 %copy-start.18 = (pred[192,2,768]{2,1,0:T(4,128)(4,1)S(1)}, pred[192,2,768]{2,1,0:T(4,128)(4,1)}, u32[]{:S(2)}) copy-start(pred[192,2,768]{2,1,0:T(4,128)(4,1)} %eq.102) | copy-start | bytes 884740
  258.6 9.5 %collective-permute-start.23 = (bf16[144,512]{1,0:T(8,128)(2,1)S(1)}, bf16[144,512]{1,0:T(8,128)(2,1)S(1)}, u32[]{:S(2)}, u32[]{:S(2)}) collective-permute-start(bf16[144,512]{1,0:T(8,128)(2,1)S(1)} %get-tuple-element.126), channel_id=1, source_target_pairs={{0,96},{8,104},{16,112},{24,120},{32,64},{40,72},{48,80},{56,88},{... | collective-permute-start | bytes 442376 | tf_op jit(solution)/shard_map/ppermute | solution.py:33
  262.3 7.8 %collective-permute-start.20 = (bf16[128,512]{1,0:T(8,128)(2,1)S(1)}, bf16[128,512]{1,0:T(8,128)(2,1)S(1)}, u32[]{:S(2)}, u32[]{:S(2)}) collective-permute-start(bf16[128,512]{1,0:T(8,128)(2,1)S(1)} %fusion.45), channel_id=1, source_target_pairs={{0,16},{8,24},{16,0},{24,8},{32,48},{40,56},{48,32},{56,40},{64,80... | collective-permute-start | bytes 393224 | tf_op jit(solution)/shard_map/ppermute | solution.py:33
  270.0 3.4 %copy-start.1 = (bf16[3,32,512]{2,1,0:T(8,128)(2,1)S(1)}, bf16[3,32,512]{2,1,0:T(8,128)(2,1)}, u32[]{:S(2)}) copy-start(bf16[3,32,512]{2,1,0:T(8,128)(2,1)} %param.11) | copy-start | bytes 294916
where the time goes:
time: 275 us; the launch traced here: 273 us
  Pallas kernels  131 us (48%)
  starting transfers between devices  46.3 us (17%)
  waiting for transfers between devices  33.6 us (12%)
  blocking collectives  22.4 us (8%)
  local copies, waits for them, and re-layouts  18.4 us (7%)
  matrix products  10.3 us (4%)
  other arithmetic  9.52 us (3%)
    pallas_call x5, Pallas kernels, attention_call(): pl.pallas_call(kernel, out_shape=out_shape, in_specs=specs * len(operands...  108 us
    ppermute x24, starting transfers between devices, hop(): lax.ppermute(value, axis, [(i, target(i) % count) for i in range(count)])  27.1 us
    all_to_all x4, waiting for transfers between devices, exchange(): lax.all_to_all(buffer, 'exp', split_axis=0, concat_axis=0, tiled=True)  23 us
    all_to_all x1, blocking collectives, exchange(): lax.all_to_all(buffer, 'exp', split_axis=0, concat_axis=0, tiled=True)  22.4 us
    all_to_all x4, starting transfers between devices, exchange(): lax.all_to_all(buffer, 'exp', split_axis=0, concat_axis=0, tiled=True)  19.1 us
    unnamed x59, local copies, waits for them, and re-layouts  12.8 us
    ppermute x24, waiting for transfers between devices, hop(): lax.ppermute(value, axis, [(i, target(i) % count) for i in range(count)])  10.7 us
    pallas_call x1, Pallas kernels, expert_forward(): pl.pallas_call(expert_forward_kernel, grid=(lane.shape[0],), out_shape=ja...  6.7 us
  transfers between devices with their start and end apart: 28, of which 10 were waited for; matrix products, arithmetic and copies ran while one was open for 5% of the time, Pallas kernels for 45%

commit v1 on v0

--- a/solution.py
+++ b/solution.py
@@ -171,7 +171,7 @@
 
 
 def near_hops(value):
-    return [hop(value, "blk", lambda i, step=step: i ^ step) for step in (2, 4, 12, 8)]
+    return [hop(value, "blk", lambda i, step=step: i ^ step) for step in (8, 12, 4, 2)]
 
 
 def attention(projected, output_weight, expert_weights, owners):
@@ -201,7 +201,7 @@
         )
 
     near, total = lax.optimization_barrier((near, total))
-    beyond = hop(jnp.concatenate(near[1:], axis=0), "blk", lambda i: i ^ 2)
+    beyond = hop(jnp.concatenate(near[:3], axis=0), "blk", lambda i: i ^ 2)
     near_partner = hop(jnp.concatenate(near, axis=0), "blk", lambda i: i ^ 1)
     total = more(total, near)
     near_partner, expert_weights, total = lax.optimization_barrier(
@@ -258,25 +258,18 @@
     ]
 
 
-def expert_forward_kernel(rows_ref, in_lane, in_partner, out_lane, out_partner, result_ref, total):
-    step = pl.program_id(0)
-    pre_act = dot_rows(rows_ref[...], tile_rows(in_lane, in_partner))
-    hidden = (pre_act * (0.5 * (1.0 + tanh_part(pre_act)))).astype(jnp.bfloat16)
-    part = jnp.dot(
-        hidden, tile_rows(out_lane, out_partner), preferred_element_type=jnp.float32
-    )
-
-    @pl.when(step == 0)
-    def _():
-        total[...] = part
-
-    @pl.when(step > 0)
-    def _():
-        total[...] += part
-
-    @pl.when(step == pl.num_programs(0) - 1)
-    def _():
-        result_ref[...] = total[...].astype(result_ref.dtype)
+def expert_forward_kernel(rows_ref, lane_ref, partner_ref, result_ref):
+    rows = rows_ref[...]
+    total = jnp.zeros(result_ref.shape, jnp.float32)
+    for step in range(lane_ref.shape[0]):
+        weights = [
+            tile_rows(lane_ref.at[step, :, which], partner_ref.at[step, :, which])
+            for which in range(2)
+        ]
+        pre_act = dot_rows(rows, weights[0])
+        hidden = (pre_act * (0.5 * (1.0 + tanh_part(pre_act)))).astype(jnp.bfloat16)
+        total += jnp.dot(hidden, weights[1], preferred_element_type=jnp.float32)
+    result_ref[...] = total.astype(result_ref.dtype)
 
 
 def expert_forward(rows, lane, partner):
@@ -284,18 +277,16 @@
     hidden = lane.size // width
     return pl.pallas_call(
         expert_forward_kernel,
-        grid=(lane.shape[0],),
         out_shape=jax.ShapeDtypeStruct((count, width), jnp.bfloat16),
-        in_specs=[pl.BlockSpec((count, width), lambda i: (0, 0)), *weight_specs(lane)],
-        out_specs=pl.BlockSpec((count, width), lambda i: (0, 0)),
-        scratch_shapes=[pltpu.VMEM((count, width), jnp.float32)],
+        in_specs=[pl.BlockSpec(memory_space=pltpu.VMEM)] * 3,
+        out_specs=pl.BlockSpec(memory_space=pltpu.VMEM),
         compiler_params=pltpu.CompilerParams(vmem_limit_bytes=EXPERT_VMEM),
         cost_estimate=pl.CostEstimate(
             flops=4 * count * width * hidden,
             transcendentals=count * hidden,
             bytes_accessed=4 * hidden * width,
         ),
-    )(rows, lane, partner, lane, partner)
+    )(rows, lane, partner)
 
 
 def expert_slopes_kernel(
@@ -316,9 +307,10 @@
     tanh = tanh_part(pre_act)
     half = 0.5 * (1.0 + tanh)
     hidden_ref[...] = (pre_act * half).astype(hidden_ref.dtype)
-    slope_ref[...] = half + pre_act * (0.5 * (1.0 - tanh * tanh)) * (
+    slope = half + pre_act * (0.5 * (1.0 - tanh * tanh)) * (
         TANH_SCALE * (1.0 + 3.0 * CUBE * (pre_act * pre_act))
     )
+    slope_ref[...] = slope.astype(slope_ref.dtype)
 
 
 def expert_slopes(rows, lane, partner):
@@ -330,7 +322,7 @@
         grid=(lane.shape[0],),
         out_shape=(
             jax.ShapeDtypeStruct((hidden, count), jnp.bfloat16),
-            jax.ShapeDtypeStruct((hidden, count), jnp.float32),
+            jax.ShapeDtypeStruct((hidden, count), jnp.bfloat16),
             jax.ShapeDtypeStruct((hidden, width), jnp.bfloat16),
             jax.ShapeDtypeStruct((width, hidden), jnp.bfloat16),
         ),
@@ -379,27 +371,15 @@
     pre_grad_ref,
 ):
     hidden_grad = dot_rows(out_weight_ref[...], routed_rows(grads_ref))
-    pre_grad = (hidden_grad * slope_ref[...]).astype(jnp.bfloat16)
+    pre_grad = (hidden_grad * slope_ref[...].astype(jnp.float32)).astype(jnp.bfloat16)
     pre_grad_ref[...] = pre_grad
     term = jnp.dot(pre_grad, rows_ref[...], preferred_element_type=jnp.float32)
     store_shares(term * scale, mine_ref, theirs_ref)
 
 
-def rows_back_kernel(pre_grad_ref, in_weight_ref, back_ref, total):
-    step = pl.program_id(0)
-    part = jnp.dot(in_weight_ref[...], pre_grad_ref[...], preferred_element_type=jnp.float32)
-
-    @pl.when(step == 0)
-    def _():
-        total[...] = part
-
-    @pl.when(step > 0)
-    def _():
-        total[...] += part
-
-    @pl.when(step == pl.num_programs(0) - 1)
-    def _():
-        back_ref[...] = total[...].T.astype(back_ref.dtype)
+def rows_back_kernel(pre_grad_ref, in_weight_ref, back_ref):
+    total = jnp.dot(in_weight_ref[...], pre_grad_ref[...], preferred_element_type=jnp.float32)
+    back_ref[...] = total.T.astype(back_ref.dtype)
 
 
 def share_shapes(hidden, width):
@@ -459,14 +439,9 @@
     width = in_weight.shape[0]
     return pl.pallas_call(
         rows_back_kernel,
-        grid=(4,),
         out_shape=jax.ShapeDtypeStruct((count, width), jnp.bfloat16),
-        in_specs=[
-            pl.BlockSpec((units // 4, count), lambda i: (i, 0)),
-            pl.BlockSpec((width, units // 4), lambda i: (0, i)),
-        ],
-        out_specs=pl.BlockSpec((count, width), lambda i: (0, 0)),
-        scratch_shapes=[pltpu.VMEM((width, count), jnp.float32)],
+        in_specs=[pl.BlockSpec(memory_space=pltpu.VMEM)] * 2,
+        out_specs=pl.BlockSpec(memory_space=pltpu.VMEM),
         compiler_params=pltpu.CompilerParams(vmem_limit_bytes=EXPERT_VMEM),
         cost_estimate=pl.CostEstimate(
             flops=units * count, transcendentals=0, bytes_accessed=count * width

time: 275 us -> 272 us (0.989)
  waiting for transfers between devices: 33.6 us -> 36.6 us
    unnamed x59 -> x51, local copies, waits for them, and re-layouts: 12.8 us -> 10.1 us
  transfers between devices with their start and end apart: 28 -> 28, of which waited for: 10 -> 10; matrix products, arithmetic and copies ran while one was open for 5% -> 7% of each run, Pallas kernels for 45% -> 45%
where the time goes in v1:
time: 272 us; the launch traced here: 271 us
  Pallas kernels  129 us (47%)
  starting transfers between devices  44.5 us (16%)
  waiting for transfers between devices  36.6 us (13%)
  blocking collectives  22.1 us (8%)
  local copies, waits for them, and re-layouts  16.4 us (6%)
  other arithmetic  11.9 us (4%)
  matrix products  9.18 us (3%)
    pallas_call x5, Pallas kernels, attention_call(): pl.pallas_call(kernel, out_shape=out_shape, in_specs=specs * len(operands...  108 us
    ppermute x24, starting transfers between devices, hop(): lax.ppermute(value, axis, [(i, target(i) % count) for i in range(count)])  26 us
    all_to_all x4, waiting for transfers between devices, exchange(): lax.all_to_all(buffer, 'exp', split_axis=0, concat_axis=0, tiled=True)  23.2 us
    all_to_all x1, blocking collectives, exchange(): lax.all_to_all(buffer, 'exp', split_axis=0, concat_axis=0, tiled=True)  22.1 us
    all_to_all x4, starting transfers between devices, exchange(): lax.all_to_all(buffer, 'exp', split_axis=0, concat_axis=0, tiled=True)  18.4 us
    ppermute x24, waiting for transfers between devices, hop(): lax.ppermute(value, axis, [(i, target(i) % count) for i in range(count)])  13.4 us
    unnamed x51, local copies, waits for them, and re-layouts  10.1 us
    pallas_call x1, Pallas kernels, expert_slopes(): pl.pallas_call(expert_slopes_kernel, grid=(lane.shape[0],), out_shape=(ja...  6.74 us
  transfers between devices with their start and end apart: 28, of which 10 were waited for; matrix products, arithmetic and copies ran while one was open for 7% of the time, Pallas kernels for 45%

profile of v1, /device:TPU:0, one launch (start us, length us, event | category | flops | bytes accessed | tf_op | source)
XLA Modules:
  0.0 271.1 jit_solution(2475555370891996572)
XLA Ops:
  0.7 0.9 copy-done
  1.5 2.0 convolution_convert_fusion.refs_0_.refs_2_
  3.7 4.0 %collective-permute-start.1 = (bf16[64,1536]{1,0:T(8,128)(2,1)S(1)}, bf16[64,1536]{1,0:T(8,128)(2,1)S(1)}, u32[]{:S(2)}, u32[]{:S(2)}) collective-permute-start(bf16[64,1536]{1,0:T(8,128)(2,1)S(1)} %slice.148), channel_id=1, source_target_pairs={{0,64},{8,72},{16,80},{24,88},{32,96},{40,104},{48,112},{56,120},{... | collective-permute-start | bytes 589832 | tf_op jit(solution)/shard_map/ppermute | solution.py:33
  7.7 0.7 collective-permute-start.2
  8.7 1.6 collective-permute-start.4
  10.7 0.9 reduce-window.6
  12.0 5.0 %shard_map.145 = (bf16[128,1536]{1,0:T(8,128)(2,1)S(1)}, f32[48,1536]{1,0:T(8,128)S(1)}) custom-call(bf16[96,1536]{1,0:T(8,128)(2,1)S(1)} %convolution_convert_fusion.refs_0_.refs_2_, bf16[64,1536]{1,0:T(8,128)(2,1)S(1)} %collective-permute-done.refs_1_.refs_5_), custom_call_target="tpu_custom_call" | custom-call | flops 5662310400 | bytes 393216 | tf_op jit(solution)/shard_map/pallas_call | solution.py:153
  17.4 0.8 collective-permute-done.3.refs_4_.refs_8_
  18.4 1.7 collective-permute-start.5
  20.1 9.7 %shard_map.146.refs_1_ = f32[48,1536]{1,0:T(8,128)S(1)} custom-call(bf16[128,1536]{1,0:T(8,128)(2,1)S(1)} %get-tuple-element.55.refs_0_, f32[48,1536]{1,0:T(8,128)S(1)} %get-tuple-element.61.refs_1_, bf16[64,1536]{1,0:T(8,128)(2,1)S(1)} %collective-permute-done.1.refs_2_.refs_6_, ...), custom_call_target="tpu_custom_call", output_to_operand_aliasing={{}: (1, {})} | custom-call | flops 11324620800 | bytes 786432 | tf_op jit(solution)/shard_map/pallas_call | solution.py:153
  30.3 9.8 %shard_map.147.refs_1_ = f32[48,1536]{1,0:T(8,128)S(1)} custom-call(bf16[128,1536]{1,0:T(8,128)(2,1)S(1)} %get-tuple-element.55.refs_0_, f32[48,1536]{1,0:T(8,128)S(1)} %shard_map.146.refs_1_, bf16[256,1536]{1,0:T(8,128)(2,1)S(1)} %collective-permute-done.6.refs_2_.refs_10_), custom_call_target="tpu_custom_call", output_to_operand_aliasing={{}: (1, {})} | custom-call | flops 11324620800 | bytes 786432 | tf_op jit(solution)/shard_map/pallas_call | solution.py:153
  40.2 1.1 collective-permute-start.9
  41.3 3.1 %collective-permute-start.10 = (bf16[2,2,128,512]{3,2,1,0:T(8,128)(2,1)S(1)}, bf16[2,2,128,512]{3,2,1,0:T(8,128)(2,1)S(1)}, u32[]{:S(2)}, u32[]{:S(2)}) collective-permute-start(bf16[2,2,128,512]{3,2,1,0:T(8,128)(2,1)S(1)} %get-tuple-element.121), channel_id=1, source_target_pairs={{0,64},{8,72},{16,80},{24,88},{32,96},{40,104},{48,112},{56,120},{... | collective-permute-start | bytes 1572872 | tf_op jit(solution)/shard_map/ppermute | solution.py:33
  44.4 0.6 collective-permute-start.11
  45.0 7.3 %shard_map.148.refs_1_ = f32[48,1536]{1,0:T(8,128)S(1)} custom-call(bf16[128,1536]{1,0:T(8,128)(2,1)S(1)} %get-tuple-element.55.refs_0_, f32[48,1536]{1,0:T(8,128)S(1)} %shard_map.147.refs_1_, bf16[192,1536]{1,0:T(8,128)(2,1)S(1)} %collective-permute-done.5.refs_2_.refs_11_), custom_call_target="tpu_custom_call", output_to_operand_aliasing={{}: (1, {})} | custom-call | flops 8493465600 | bytes 589824 | tf_op jit(solution)/shard_map/pallas_call | solution.py:153
  52.4 75.7 %shard_map.149 = bf16[8,32,704]{2,1,0:T(8,128)(2,1)} custom-call(bf16[128,1536]{1,0:T(8,128)(2,1)S(1)} %get-tuple-element.55.refs_0_, f32[48,1536]{1,0:T(8,128)S(1)} %shard_map.148.refs_1_, bf16[96,1536]{1,0:T(8,128)(2,1)S(1)} %convolution_convert_fusion.refs_0_.refs_2_, bf16[32,512]{1,0:T(8,128)(2,1)S(1)} %copy-done.10, ...), custom_call_target="tpu_custom_call" | custom-call | flops 8493465600 | bytes 589824 | tf_op jit(solution)/shard_map/pallas_call | solution.py:153
  128.1 6.9 %all-to-all-start = ((bf16[8,32,704]{2,1,0:T(8,128)(2,1)}), bf16[8,32,704]{2,1,0:T(8,128)(2,1)S(1)}, u32[]{:S(2)}, u32[]{:S(2)}) async-start(bf16[8,32,704]{2,1,0:T(8,128)(2,1)} %shard_map.149), calls=%async_computation | async-start | bytes 786432 | tf_op jit(solution)/shard_map/all_to_all | solution.py:28
  135.1 0.8 copy-done.17
  136.1 1.6 pad_maximum_fusion.lane_ref.in_lane.out_lane
  137.7 8.2 %all-to-all-done = bf16[8,32,704]{2,1,0:T(8,128)(2,1)S(1)} async-done(((bf16[8,32,704]{2,1,0:T(8,128)(2,1)}), bf16[8,32,704]{2,1,0:T(8,128)(2,1)S(1)}, u32[]{:S(2)}, u32[]{:S(2)}) %all-to-all-start) | async-done | bytes 360480 | tf_op jit(solution)/shard_map/all_to_all | solution.py:28
  145.9 1.3 multiply_reduce_fusion.2
  147.2 0.8 copy-done.13
  148.5 1.5 convolution_convert_fusion.1
  149.9 3.5 %all-to-all-start.1 = ((bf16[8,96,512]{2,1,0:T(8,128)(2,1)}), bf16[8,96,512]{2,1,0:T(8,128)(2,1)S(1)}, u32[]{:S(2)}, u32[]{:S(2)}) async-start(bf16[8,96,512]{2,1,0:T(8,128)(2,1)} %bitcast.115), calls=%async_computation.1 | async-start | bytes 1572864 | tf_op jit(solution)/shard_map/all_to_all | solution.py:28
  154.0 14.8 %all-to-all-done.1 = bf16[8,96,512]{2,1,0:T(8,128)(2,1)S(1)} async-done(((bf16[8,96,512]{2,1,0:T(8,128)(2,1)}), bf16[8,96,512]{2,1,0:T(8,128)(2,1)S(1)}, u32[]{:S(2)}, u32[]{:S(2)}) %all-to-all-start.1) | async-done | bytes 786464 | tf_op jit(solution)/shard_map/all_to_all | solution.py:28
  168.8 5.6 %shard_map.150 = bf16[768,512]{1,0:T(8,128)(2,1)S(1)} custom-call(bf16[768,512]{1,0:T(8,128)(2,1)S(1)} %bitcast.106, bf16[4,2,2,128,512]{4,3,2,1,0:T(8,128)(2,1)S(1)} %pad_maximum_fusion.lane_ref.in_lane.out_lane, bf16[4,2,2,128,512]{4,3,2,1,0:T(8,128)(2,1)} %collective-permute-done.12.partner_ref.in_partner.out_partner), custom_call_target="tpu_custom_call" | custom-call | flops 3221225472 | bytes 4194304 | tf_op jit(solution)/shard_map/pallas_call | solution.py:278
  174.4 0.9 copy-done.3
  175.3 4.4 %all-to-all-start.2 = ((bf16[8,96,512]{2,1,0:T(8,128)(2,1)}), bf16[8,96,512]{2,1,0:T(8,128)(2,1)}, u32[]{:S(2)}, u32[]{:S(2)}) async-start(bf16[8,96,512]{2,1,0:T(8,128)(2,1)} %bitcast.109), calls=%async_computation.2 | async-start | bytes 1572864 | tf_op jit(solution)/shard_map/all_to_all | solution.py:28
  179.8 1.1 eq.102
  181.2 6.7 %shard_map.151 = (bf16[2048,768]{1,0:T(8,128)(2,1)S(1)}, bf16[2048,768]{1,0:T(8,128)(2,1)S(1)}, bf16[2048,512]{1,0:T(8,128)(2,1)S(1)}, bf16[512,2048]{1,0:T(8,128)(2,1)S(1)}) custom-call(bf16[768,512]{1,0:T(8,128)(2,1)S(1)} %bitcast.107, bf16[4,2,2,128,512]{4,3,2,1,0:T(8,128)(2,1)S(1)} %pad_maximum_fusion.lane_ref.in_lane.out_lane, ...), custom_call_target="tpu_custom_call" | custom-call | flops 1610612736 | bytes 17825792 | tf_op jit(solution)/shard_map/pallas_call | solution.py:320
  188.0 1.4 copy-done.1
  189.3 1.6 copy-done.4
  191.0 1.7 copy-done.6
  192.6 1.4 copy-done.8
  194.2 1.8 fusion.37
  196.5 0.8 add_add_fusion
  197.8 0.5 mul.202
  198.8 0.8 fusion.5
  199.6 22.1 %all_to_all.25.refs_1_.refs_3_ = bf16[8,112,512]{2,1,0:T(8,128)(2,1)S(1)} all-to-all(bf16[8,112,512]{2,1,0:T(8,128)(2,1)S(1)} %bitcast.113), channel_id=1, replica_groups=mesh['blk'=16,'exp'=8] {'exp'}, dimensions={0} | all-to-all | bytes 1835008 | tf_op jit(solution)/shard_map/all_to_all | solution.py:28
  221.7 2.3 shard_map.152
  224.3 4.1 %shard_map.153 = (f32[4,2,128,512]{3,2,1,0:T(8,128)S(1)}, bf16[4,2,128,512]{3,2,1,0:T(8,128)(2,1)S(1)}, bf16[2048,768]{1,0:T(8,128)(2,1)S(1)}) custom-call(bf16[2048,768]{1,0:T(8,128)(2,1)S(1)} %copy-done.5, bf16[2048,512]{1,0:T(8,128)(2,1)S(1)} %copy-done.9, bf16[768,512]{1,0:T(8,128)(2,1)S(1)} %bitcast.108, bf16[8,112,512]{2,1,0:T(8,128)(2,1)S(1)} %all_to_all.25.refs_1_.refs_3_), custom_call_target="tpu_custom_call" | custom-call | flops 3221225472 | bytes 9437184 | tf_op jit(solution)/shard_map/pallas_call | solution.py:419
  229.1 2.1 collective-permute-done.13
  231.6 0.8 pad_maximum_fusion.3
  232.5 0.7 collective-permute-start.16
  233.3 2.7 %shard_map.154 = bf16[768,512]{1,0:T(8,128)(2,1)} custom-call(bf16[2048,768]{1,0:T(8,128)(2,1)S(1)} %get-tuple-element.92.pre_grad_ref, bf16[512,2048]{1,0:T(8,128)(2,1)S(1)} %copy-done.2), custom_call_target="tpu_custom_call" | custom-call | flops 1572864 | bytes 393216 | tf_op jit(solution)/shard_map/pallas_call | solution.py:440
  236.1 1.8 fusion.72
  237.9 0.9 slice_bitcast_fusion.6
  238.8 4.1 %collective-permute-start.18 = (bf16[2,128,512]{2,1,0:T(8,128)(2,1)}, bf16[2,128,512]{2,1,0:T(8,128)(2,1)}, u32[]{:S(2)}, u32[]{:S(2)}) collective-permute-start(bf16[2,128,512]{2,1,0:T(8,128)(2,1)} %get-tuple-element.116), channel_id=1, source_target_pairs={{0,64},{8,72},{16,80},{24,88},{32,96},{40,104},{48,112},{56,120},{... | collective-permute-start | bytes 786440 | tf_op jit(solution)/shard_map/ppermute | solution.py:33
  242.8 0.6 collective-permute-start.19
  243.5 3.5 %all-to-all-start.4 = ((bf16[8,96,512]{2,1,0:T(8,128)(2,1)}), bf16[8,96,512]{2,1,0:T(8,128)(2,1)S(1)}, u32[]{:S(2)}, u32[]{:S(2)}) async-start(bf16[8,96,512]{2,1,0:T(8,128)(2,1)} %bitcast.22), calls=%async_computation.4 | async-start | bytes 1572864 | tf_op jit(solution)/shard_map/all_to_all | solution.py:28
  247.3 1.1 slice.130
  248.7 0.7 add_convert_fusion
  249.6 4.1 %collective-permute-start.22 = (bf16[144,512]{1,0:T(8,128)(2,1)S(1)}, bf16[144,512]{1,0:T(8,128)(2,1)S(1)}, u32[]{:S(2)}, u32[]{:S(2)}) collective-permute-start(bf16[144,512]{1,0:T(8,128)(2,1)S(1)} %get-tuple-element.125), channel_id=1, source_target_pairs={{0,64},{8,72},{16,80},{24,88},{32,96},{40,104},{48,112},{56,120},{... | collective-permute-start | bytes 442376 | tf_op jit(solution)/shard_map/ppermute | solution.py:33
  253.6 0.6 collective-permute-start.23
  254.2 1.7 collective-permute-done.18
  255.9 6.4 %collective-permute-done.19 = bf16[2,128,512]{2,1,0:T(8,128)(2,1)} collective-permute-done((bf16[2,128,512]{2,1,0:T(8,128)(2,1)}, bf16[2,128,512]{2,1,0:T(8,128)(2,1)}, u32[]{:S(2)}, u32[]{:S(2)}) %collective-permute-start.19) | collective-permute-done | bytes 262176 | tf_op jit(solution)/shard_map/ppermute | solution.py:33
  262.4 1.4 bitcast_add_fusion
  263.8 1.3 collective-permute-start.20
  265.1 0.6 slice.172
  265.7 0.6 slice.173
  266.3 0.8 fusion.42
  267.1 1.8 collective-permute-done.20
  268.8 0.7 fusion.40
  270.1 1.1 fusion.9
  (127 shorter events, 8.0 us)
Async XLA Ops:
  0.6 0.9 copy-start
  0.6 9.7 %copy-start.22 = (s32[192,2]{0,1:T(2,128)S(1)}, s32[192,2]{0,1:T(2,128)}, u32[]{:S(2)}) copy-start(s32[192,2]{0,1:T(2,128)} %param.18) | copy-start | bytes 4612
  0.7 11.3 %copy-start.20 = (bf16[1,128,512]{2,1,0:T(8,128)(2,1)S(1)}, bf16[1,128,512]{2,1,0:T(8,128)(2,1)}, u32[]{:S(2)}) copy-start(bf16[1,128,512]{2,1,0:T(8,128)(2,1)} %param.16) | copy-start | bytes 393220
  0.7 11.3 %copy-start.19 = (bf16[1,128,512]{2,1,0:T(8,128)(2,1)S(1)}, bf16[1,128,512]{2,1,0:T(8,128)(2,1)}, u32[]{:S(2)}) copy-start(bf16[1,128,512]{2,1,0:T(8,128)(2,1)} %param.17) | copy-start | bytes 393220
  3.6 8.4 %collective-permute-start = (bf16[64,1536]{1,0:T(8,128)(2,1)S(1)}, bf16[64,1536]{1,0:T(8,128)(2,1)S(1)}, u32[]{:S(2)}, u32[]{:S(2)}) collective-permute-start(bf16[64,1536]{1,0:T(8,128)(2,1)S(1)} %slice.148), channel_id=1, source_target_pairs={{0,8},{8,0},{16,24},{24,16},{32,40},{40,32},{48,56},{56,48},{64,72... | collective-permute-start | bytes 589832 | tf_op jit(solution)/shard_map/ppermute | solution.py:33
  3.7 13.4 %collective-permute-start.1 = (bf16[64,1536]{1,0:T(8,128)(2,1)S(1)}, bf16[64,1536]{1,0:T(8,128)(2,1)S(1)}, u32[]{:S(2)}, u32[]{:S(2)}) collective-permute-start(bf16[64,1536]{1,0:T(8,128)(2,1)S(1)} %slice.148), channel_id=1, source_target_pairs={{0,64},{8,72},{16,80},{24,88},{32,96},{40,104},{48,112},{56,120},{... | collective-permute-start | bytes 589832 | tf_op jit(solution)/shard_map/ppermute | solution.py:33
  7.7 9.7 %collective-permute-start.2 = (bf16[64,1536]{1,0:T(8,128)(2,1)S(1)}, bf16[64,1536]{1,0:T(8,128)(2,1)S(1)}, u32[]{:S(2)}, u32[]{:S(2)}) collective-permute-start(bf16[64,1536]{1,0:T(8,128)(2,1)S(1)} %slice.148), channel_id=1, source_target_pairs={{0,96},{8,104},{16,112},{24,120},{32,64},{40,72},{48,80},{56,88},{... | collective-permute-start | bytes 589832 | tf_op jit(solution)/shard_map/ppermute | solution.py:33
  8.4 9.8 %collective-permute-start.3 = (bf16[64,1536]{1,0:T(8,128)(2,1)S(1)}, bf16[64,1536]{1,0:T(8,128)(2,1)S(1)}, u32[]{:S(2)}, u32[]{:S(2)}) collective-permute-start(bf16[64,1536]{1,0:T(8,128)(2,1)S(1)} %slice.148), channel_id=1, source_target_pairs={{0,32},{8,40},{16,48},{24,56},{32,0},{40,8},{48,16},{56,24},{64,96... | collective-permute-start | bytes 589832 | tf_op jit(solution)/shard_map/ppermute | solution.py:33
  8.7 9.5 %collective-permute-start.4 = (bf16[64,1536]{1,0:T(8,128)(2,1)S(1)}, bf16[64,1536]{1,0:T(8,128)(2,1)S(1)}, u32[]{:S(2)}, u32[]{:S(2)}) collective-permute-start(bf16[64,1536]{1,0:T(8,128)(2,1)S(1)} %slice.148), channel_id=1, source_target_pairs={{0,16},{8,24},{16,0},{24,8},{32,48},{40,56},{48,32},{56,40},{64,80... | collective-permute-start | bytes 589832 | tf_op jit(solution)/shard_map/ppermute | solution.py:33
  18.3 11.5 %collective-permute-start.6 = (bf16[256,1536]{1,0:T(8,128)(2,1)S(1)}, bf16[256,1536]{1,0:T(8,128)(2,1)S(1)}, u32[]{:S(2)}, u32[]{:S(2)}) collective-permute-start(bf16[256,1536]{1,0:T(8,128)(2,1)S(1)} %pad_maximum_fusion.1), channel_id=1, source_target_pairs={{0,8},{8,0},{16,24},{24,16},{32,40},{40,32},{48,56},{56,48},{64,72... | collective-permute-start | bytes 2359304 | tf_op jit(solution)/shard_map/ppermute | solution.py:33
  18.4 21.7 %collective-permute-start.5 = (bf16[192,1536]{1,0:T(8,128)(2,1)S(1)}, bf16[192,1536]{1,0:T(8,128)(2,1)S(1)}, u32[]{:S(2)}, u32[]{:S(2)}) collective-permute-start(bf16[192,1536]{1,0:T(8,128)(2,1)S(1)} %pad_maximum_fusion.2), channel_id=1, source_target_pairs={{0,16},{8,24},{16,0},{24,8},{32,48},{40,56},{48,32},{56,40},{64,80... | collective-permute-start | bytes 1769480 | tf_op jit(solution)/shard_map/ppermute | solution.py:33
  29.8 10.3 %collective-permute-start.7 = (bf16[2,128,512]{2,1,0:T(8,128)(2,1)S(1)}, bf16[2,128,512]{2,1,0:T(8,128)(2,1)S(1)}, u32[]{:S(2)}, u32[]{:S(2)}) collective-permute-start(bf16[2,128,512]{2,1,0:T(8,128)(2,1)S(1)} %pad_maximum_fusion.5), channel_id=1, source_target_pairs={{0,16},{8,24},{16,0},{24,8},{32,48},{40,56},{48,32},{56,40},{64,80... | collective-permute-start | bytes 786440 | tf_op jit(solution)/shard_map/ppermute | solution.py:33
  40.2 12.2 %copy-start.10 = (bf16[32,512]{1,0:T(8,128)(2,1)S(1)}, bf16[32,512]{1,0:T(8,128)(2,1)}, u32[]{:S(2)}) copy-start(bf16[32,512]{1,0:T(8,128)(2,1)} %refs_3_.1) | copy-start | bytes 98308
  40.2 94.8 %collective-permute-start.9 = (bf16[2,2,128,512]{3,2,1,0:T(8,128)(2,1)S(1)}, bf16[2,2,128,512]{3,2,1,0:T(8,128)(2,1)S(1)}, u32[]{:S(2)}, u32[]{:S(2)}) collective-permute-start(bf16[2,2,128,512]{3,2,1,0:T(8,128)(2,1)S(1)} %get-tuple-element.121), channel_id=1, source_target_pairs={{0,32},{8,40},{16,48},{24,56},{32,0},{40,8},{48,16},{56,24},{64,96... | collective-permute-start | bytes 1572872 | tf_op jit(solution)/shard_map/ppermute | solution.py:33
  41.3 93.8 %collective-permute-start.10 = (bf16[2,2,128,512]{3,2,1,0:T(8,128)(2,1)S(1)}, bf16[2,2,128,512]{3,2,1,0:T(8,128)(2,1)S(1)}, u32[]{:S(2)}, u32[]{:S(2)}) collective-permute-start(bf16[2,2,128,512]{3,2,1,0:T(8,128)(2,1)S(1)} %get-tuple-element.121), channel_id=1, source_target_pairs={{0,64},{8,72},{16,80},{24,88},{32,96},{40,104},{48,112},{56,120},{... | collective-permute-start | bytes 1572872 | tf_op jit(solution)/shard_map/ppermute | solution.py:33
  44.4 90.7 %collective-permute-start.11 = (bf16[2,2,128,512]{3,2,1,0:T(8,128)(2,1)S(1)}, bf16[2,2,128,512]{3,2,1,0:T(8,128)(2,1)}, u32[]{:S(2)}, u32[]{:S(2)}) collective-permute-start(bf16[2,2,128,512]{3,2,1,0:T(8,128)(2,1)S(1)} %get-tuple-element.121), channel_id=1, source_target_pairs={{0,96},{8,104},{16,112},{24,120},{32,64},{40,72},{48,80},{56,88},{... | collective-permute-start | bytes 1572872 | tf_op jit(solution)/shard_map/ppermute | solution.py:33
  45.0 7.4 %collective-permute-start.8 = (bf16[192,1536]{1,0:T(8,128)(2,1)S(1)}, bf16[192,1536]{1,0:T(8,128)(2,1)S(1)}, u32[]{:S(2)}, u32[]{:S(2)}) collective-permute-start(bf16[192,1536]{1,0:T(8,128)(2,1)S(1)} %collective-permute-done.5.refs_2_.refs_11_), channel_id=1, source_target_pairs={{0,8},{8,0},{16,24},{24,16},{32,40},{40,32},{48,56},{56,48},{64,72... | collective-permute-start | bytes 1769480 | tf_op jit(solution)/shard_map/ppermute | solution.py:33
  128.1 17.8 %all-to-all-start = ((bf16[8,32,704]{2,1,0:T(8,128)(2,1)}), bf16[8,32,704]{2,1,0:T(8,128)(2,1)S(1)}, u32[]{:S(2)}, u32[]{:S(2)}) async-start(bf16[8,32,704]{2,1,0:T(8,128)(2,1)} %shard_map.149), calls=%async_computation | async-start | bytes 786432 | tf_op jit(solution)/shard_map/all_to_all | solution.py:28
  135.1 0.8 copy-start.17
  135.1 1.0 copy-start.18
  136.1 11.9 %copy-start.23 = (f32[512]{0:T(512)S(1)}, f32[512]{0:T(512)}, u32[]{:S(2)}) copy-start(f32[512]{0:T(512)} %param.14) | copy-start | bytes 6148
  145.9 22.9 %collective-permute-start.12 = (bf16[4,2,2,128,512]{4,3,2,1,0:T(8,128)(2,1)S(1)}, bf16[4,2,2,128,512]{4,3,2,1,0:T(8,128)(2,1)}, u32[]{:S(2)}, u32[]{:S(2)}) collective-permute-start(bf16[4,2,2,128,512]{4,3,2,1,0:T(8,128)(2,1)S(1)} %pad_maximum_fusion.lane_ref.in_lane.out_lane), channel_id=1, source_target_pairs={{0,8},{8,0},{16,24},{24,16},{32,40},{40,32},{48,56},{56,48},{64,72... | collective-permute-start | bytes 6291464 | tf_op jit(solution)/shard_map/ppermute | solution.py:33
  147.2 0.8 copy-start.13
  148.1 5.5 %copy-start.11 = (bf16[192,512]{1,0:T(8,128)(2,1)}, bf16[192,512]{1,0:T(8,128)(2,1)S(1)}, u32[]{:S(2)}) copy-start(bf16[192,512]{1,0:T(8,128)(2,1)S(1)} %multiply_convert_fusion.2) | copy-start | bytes 589828
  148.3 5.2 %copy-start.21 = (bf16[8,512]{1,0:T(8,128)(2,1)S(1)}, bf16[8,512]{1,0:T(8,128)(2,1)}, u32[]{:S(2)}) copy-start(bf16[8,512]{1,0:T(8,128)(2,1)} %param.13) | copy-start | bytes 24580
  149.9 18.8 %all-to-all-start.1 = ((bf16[8,96,512]{2,1,0:T(8,128)(2,1)}), bf16[8,96,512]{2,1,0:T(8,128)(2,1)S(1)}, u32[]{:S(2)}, u32[]{:S(2)}) async-start(bf16[8,96,512]{2,1,0:T(8,128)(2,1)} %bitcast.115), calls=%async_computation.1 | async-start | bytes 1572864 | tf_op jit(solution)/shard_map/all_to_all | solution.py:28
  174.4 0.9 copy-start.3
  175.3 18.9 %all-to-all-start.2 = ((bf16[8,96,512]{2,1,0:T(8,128)(2,1)}), bf16[8,96,512]{2,1,0:T(8,128)(2,1)}, u32[]{:S(2)}, u32[]{:S(2)}) async-start(bf16[8,96,512]{2,1,0:T(8,128)(2,1)} %bitcast.109), calls=%async_computation.2 | async-start | bytes 1572864 | tf_op jit(solution)/shard_map/all_to_all | solution.py:28
  187.9 1.4 copy-start.1
  189.3 1.6 copy-start.4
  191.0 1.7 copy-start.6
  192.6 1.4 copy-start.8
  194.0 2.0 copy-start.14
  194.2 2.1 copy-start.15
  194.2 2.1 copy-start.24
  197.5 0.9 copy-start.12
  198.8 22.9 %copy-start.7 = (bf16[2048,768]{1,0:T(8,128)(2,1)S(1)}, bf16[2048,768]{1,0:T(8,128)(2,1)}, u32[]{:S(2)}) copy-start(bf16[2048,768]{1,0:T(8,128)(2,1)} %copy-done.6) | copy-start | bytes 9437188
  221.7 2.4 copy-start.5
  221.7 2.5 copy-start.9
  224.1 7.1 %collective-permute-start.14 = (bf16[4,2,128,512]{3,2,1,0:T(8,128)(2,1)S(1)}, bf16[4,2,128,512]{3,2,1,0:T(8,128)(2,1)S(1)}, u32[]{:S(2)}, u32[]{:S(2)}) collective-permute-start(bf16[4,2,128,512]{3,2,1,0:T(8,128)(2,1)S(1)} %get-tuple-element.81), channel_id=1, source_target_pairs={{0,8},{8,0},{16,24},{24,16},{32,40},{40,32},{48,56},{56,48},{64,72... | collective-permute-start | bytes 3145736 | tf_op jit(solution)/shard_map/ppermute | solution.py:33
  228.4 7.7 %collective-permute-start.15 = (bf16[4,2,128,512]{3,2,1,0:T(8,128)(2,1)S(1)}, bf16[4,2,128,512]{3,2,1,0:T(8,128)(2,1)S(1)}, u32[]{:S(2)}, u32[]{:S(2)}) collective-permute-start(bf16[4,2,128,512]{3,2,1,0:T(8,128)(2,1)S(1)} %get-tuple-element.87), channel_id=1, source_target_pairs={{0,8},{8,0},{16,24},{24,16},{32,40},{40,32},{48,56},{56,48},{64,72... | collective-permute-start | bytes 3145736 | tf_op jit(solution)/shard_map/ppermute | solution.py:33
  228.8 2.3 collective-permute-start.13
  231.5 1.8 copy-start.2
  232.5 14.9 %collective-permute-start.16 = (bf16[528,512]{1,0:T(8,128)(2,1)}, bf16[528,512]{1,0:T(8,128)(2,1)}, u32[]{:S(2)}, u32[]{:S(2)}) collective-permute-start(bf16[528,512]{1,0:T(8,128)(2,1)} %pad_maximum_fusion.3), channel_id=1, source_target_pairs={{0,16},{8,24},{16,0},{24,8},{32,48},{40,56},{48,32},{56,40},{64,80... | collective-permute-start | bytes 1622024 | tf_op jit(solution)/shard_map/ppermute | solution.py:33
  238.8 14.9 %collective-permute-start.17 = (bf16[2,128,512]{2,1,0:T(8,128)(2,1)}, bf16[2,128,512]{2,1,0:T(8,128)(2,1)}, u32[]{:S(2)}, u32[]{:S(2)}) collective-permute-start(bf16[2,128,512]{2,1,0:T(8,128)(2,1)} %get-tuple-element.114), channel_id=1, source_target_pairs={{0,32},{8,40},{16,48},{24,56},{32,0},{40,8},{48,16},{56,24},{64,96... | collective-permute-start | bytes 786440 | tf_op jit(solution)/shard_map/ppermute | solution.py:33
  238.8 17.2 %collective-permute-start.18 = (bf16[2,128,512]{2,1,0:T(8,128)(2,1)}, bf16[2,128,512]{2,1,0:T(8,128)(2,1)}, u32[]{:S(2)}, u32[]{:S(2)}) collective-permute-start(bf16[2,128,512]{2,1,0:T(8,128)(2,1)} %get-tuple-element.116), channel_id=1, source_target_pairs={{0,64},{8,72},{16,80},{24,88},{32,96},{40,104},{48,112},{56,120},{... | collective-permute-start | bytes 786440 | tf_op jit(solution)/shard_map/ppermute | solution.py:33
  242.8 19.5 %collective-permute-start.19 = (bf16[2,128,512]{2,1,0:T(8,128)(2,1)}, bf16[2,128,512]{2,1,0:T(8,128)(2,1)}, u32[]{:S(2)}, u32[]{:S(2)}) collective-permute-start(bf16[2,128,512]{2,1,0:T(8,128)(2,1)} %get-tuple-element.115), channel_id=1, source_target_pairs={{0,96},{8,104},{16,112},{24,120},{32,64},{40,72},{48,80},{56,88},{... | collective-permute-start | bytes 786440 | tf_op jit(solution)/shard_map/ppermute | solution.py:33
  243.5 25.4 %all-to-all-start.4 = ((bf16[8,96,512]{2,1,0:T(8,128)(2,1)}), bf16[8,96,512]{2,1,0:T(8,128)(2,1)S(1)}, u32[]{:S(2)}, u32[]{:S(2)}) async-start(bf16[8,96,512]{2,1,0:T(8,128)(2,1)} %bitcast.22), calls=%async_computation.4 | async-start | bytes 1572864 | tf_op jit(solution)/shard_map/all_to_all | solution.py:28
  249.5 15.6 %collective-permute-start.21 = (bf16[144,512]{1,0:T(8,128)(2,1)S(1)}, bf16[144,512]{1,0:T(8,128)(2,1)S(1)}, u32[]{:S(2)}, u32[]{:S(2)}) collective-permute-start(bf16[144,512]{1,0:T(8,128)(2,1)S(1)} %get-tuple-element.124), channel_id=1, source_target_pairs={{0,32},{8,40},{16,48},{24,56},{32,0},{40,8},{48,16},{56,24},{64,96... | collective-permute-start | bytes 442376 | tf_op jit(solution)/shard_map/ppermute | solution.py:33
  249.6 15.5 %collective-permute-start.22 = (bf16[144,512]{1,0:T(8,128)(2,1)S(1)}, bf16[144,512]{1,0:T(8,128)(2,1)S(1)}, u32[]{:S(2)}, u32[]{:S(2)}) collective-permute-start(bf16[144,512]{1,0:T(8,128)(2,1)S(1)} %get-tuple-element.125), channel_id=1, source_target_pairs={{0,64},{8,72},{16,80},{24,88},{32,96},{40,104},{48,112},{56,120},{... | collective-permute-start | bytes 442376 | tf_op jit(solution)/shard_map/ppermute | solution.py:33
  253.6 16.0 %copy-start.16 = (pred[192,2,768]{2,1,0:T(4,128)(4,1)S(1)}, pred[192,2,768]{2,1,0:T(4,128)(4,1)}, u32[]{:S(2)}) copy-start(pred[192,2,768]{2,1,0:T(4,128)(4,1)} %eq.102) | copy-start | bytes 884740
  253.6 11.5 %collective-permute-start.23 = (bf16[144,512]{1,0:T(8,128)(2,1)S(1)}, bf16[144,512]{1,0:T(8,128)(2,1)S(1)}, u32[]{:S(2)}, u32[]{:S(2)}) collective-permute-start(bf16[144,512]{1,0:T(8,128)(2,1)S(1)} %get-tuple-element.126), channel_id=1, source_target_pairs={{0,96},{8,104},{16,112},{24,120},{32,64},{40,72},{48,80},{56,88},{... | collective-permute-start | bytes 442376 | tf_op jit(solution)/shard_map/ppermute | solution.py:33
  263.8 5.0 %collective-permute-start.20 = (bf16[128,512]{1,0:T(8,128)(2,1)S(1)}, bf16[128,512]{1,0:T(8,128)(2,1)S(1)}, u32[]{:S(2)}, u32[]{:S(2)}) collective-permute-start(bf16[128,512]{1,0:T(8,128)(2,1)S(1)} %fusion.45), channel_id=1, source_target_pairs={{0,16},{8,24},{16,0},{24,8},{32,48},{40,56},{48,32},{56,40},{64,80... | collective-permute-start | bytes 393224 | tf_op jit(solution)/shard_map/ppermute | solution.py:33

commit v2 on v1

--- a/solution.py
+++ b/solution.py
@@ -590,12 +590,13 @@
     out_sums = out_mine + out_swapped.astype(jnp.float32)
     out_sent = add_rows(out_sums[:, 1].astype(jnp.bfloat16), sum_rows)
     out_beside = swap(out_sent, 2)
-    out_sent, out_sums, pre_grad = lax.optimization_barrier((out_sent, out_sums, pre_grad))
-    row_grads = rows_back(pre_grad, in_weight)
-    in_mine, in_swapped, row_grads = lax.optimization_barrier((in_mine, in_swapped, row_grads))
-    back_home = exchange(row_grads.reshape(experts, capacity, width))
     in_sums = in_mine + in_swapped.astype(jnp.float32)
     in_parts = swap_over_z(in_sums)
+    out_sent, out_sums, in_sums, pre_grad = lax.optimization_barrier(
+        (out_sent, out_sums, in_sums, pre_grad)
+    )
+    row_grads = rows_back(pre_grad, in_weight)
+    back_home = exchange(row_grads.reshape(experts, capacity, width))
     out_beside, in_sums = lax.optimization_barrier((out_beside, in_sums))
     sum_rows = (
         out_sent[-SUM_ROWS:].astype(jnp.float32) + out_beside[-SUM_ROWS:].astype(jnp.float32)

time: 272 us -> 267 us (0.982)
  waiting for transfers between devices: 36.6 us -> 32 us
    ppermute x24, waiting for transfers between devices: 13.4 us -> 8.82 us  [hop(): lax.ppermute(value, axis, [(i, target(i) % count) for i in range(count)])]
where the time goes in v2:
time: 267 us; the launch traced here: 266 us
  Pallas kernels  129 us (48%)
  starting transfers between devices  44.6 us (17%)
  waiting for transfers between devices  32 us (12%)
  blocking collectives  22.1 us (8%)
  local copies, waits for them, and re-layouts  16.2 us (6%)
  other arithmetic  11.9 us (4%)
  matrix products  9.18 us (3%)
    pallas_call x5, Pallas kernels, attention_call(): pl.pallas_call(kernel, out_shape=out_shape, in_specs=specs * len(operands...  108 us
    ppermute x24, starting transfers between devices, hop(): lax.ppermute(value, axis, [(i, target(i) % count) for i in range(count)])  26.1 us
    all_to_all x4, waiting for transfers between devices, exchange(): lax.all_to_all(buffer, 'exp', split_axis=0, concat_axis=0, tiled=True)  23.2 us
    all_to_all x1, blocking collectives, exchange(): lax.all_to_all(buffer, 'exp', split_axis=0, concat_axis=0, tiled=True)  22.1 us
    all_to_all x4, starting transfers between devices, exchange(): lax.all_to_all(buffer, 'exp', split_axis=0, concat_axis=0, tiled=True)  18.4 us
    unnamed x51, local copies, waits for them, and re-layouts  9.9 us
    ppermute x24, waiting for transfers between devices, hop(): lax.ppermute(value, axis, [(i, target(i) % count) for i in range(count)])  8.82 us
    pallas_call x1, Pallas kernels, expert_slopes(): pl.pallas_call(expert_slopes_kernel, grid=(lane.shape[0],), out_shape=(ja...  6.74 us
  transfers between devices with their start and end apart: 28, of which 10 were waited for; matrix products, arithmetic and copies ran while one was open for 7% of the time, Pallas kernels for 45%

profile of v2, /device:TPU:0, one launch (start us, length us, event | category | flops | bytes accessed | tf_op | source)
XLA Modules:
  0.0 266.5 jit_solution(2980623964348126268)
XLA Ops:
  0.7 0.9 copy-done
  1.5 2.0 convolution_convert_fusion.refs_0_.refs_2_
  3.7 4.0 %collective-permute-start.1 = (bf16[64,1536]{1,0:T(8,128)(2,1)S(1)}, bf16[64,1536]{1,0:T(8,128)(2,1)S(1)}, u32[]{:S(2)}, u32[]{:S(2)}) collective-permute-start(bf16[64,1536]{1,0:T(8,128)(2,1)S(1)} %slice.148), channel_id=1, source_target_pairs={{0,64},{8,72},{16,80},{24,88},{32,96},{40,104},{48,112},{56,120},{... | collective-permute-start | bytes 589832 | tf_op jit(solution)/shard_map/ppermute | solution.py:33
  7.7 0.7 collective-permute-start.2
  8.7 1.6 collective-permute-start.4
  10.7 0.9 reduce-window.6
  12.0 5.0 %shard_map.145 = (bf16[128,1536]{1,0:T(8,128)(2,1)S(1)}, f32[48,1536]{1,0:T(8,128)S(1)}) custom-call(bf16[96,1536]{1,0:T(8,128)(2,1)S(1)} %convolution_convert_fusion.refs_0_.refs_2_, bf16[64,1536]{1,0:T(8,128)(2,1)S(1)} %collective-permute-done.refs_1_.refs_5_), custom_call_target="tpu_custom_call" | custom-call | flops 5662310400 | bytes 393216 | tf_op jit(solution)/shard_map/pallas_call | solution.py:153
  17.4 0.8 collective-permute-done.3.refs_4_.refs_8_
  18.4 1.7 collective-permute-start.5
  20.1 9.7 %shard_map.146.refs_1_ = f32[48,1536]{1,0:T(8,128)S(1)} custom-call(bf16[128,1536]{1,0:T(8,128)(2,1)S(1)} %get-tuple-element.53.refs_0_, f32[48,1536]{1,0:T(8,128)S(1)} %get-tuple-element.59.refs_1_, bf16[64,1536]{1,0:T(8,128)(2,1)S(1)} %collective-permute-done.1.refs_2_.refs_6_, ...), custom_call_target="tpu_custom_call", output_to_operand_aliasing={{}: (1, {})} | custom-call | flops 11324620800 | bytes 786432 | tf_op jit(solution)/shard_map/pallas_call | solution.py:153
  30.3 9.8 %shard_map.147.refs_1_ = f32[48,1536]{1,0:T(8,128)S(1)} custom-call(bf16[128,1536]{1,0:T(8,128)(2,1)S(1)} %get-tuple-element.53.refs_0_, f32[48,1536]{1,0:T(8,128)S(1)} %shard_map.146.refs_1_, bf16[256,1536]{1,0:T(8,128)(2,1)S(1)} %collective-permute-done.6.refs_2_.refs_10_), custom_call_target="tpu_custom_call", output_to_operand_aliasing={{}: (1, {})} | custom-call | flops 11324620800 | bytes 786432 | tf_op jit(solution)/shard_map/pallas_call | solution.py:153
  40.2 1.1 collective-permute-start.9
  41.3 3.1 %collective-permute-start.10 = (bf16[2,2,128,512]{3,2,1,0:T(8,128)(2,1)S(1)}, bf16[2,2,128,512]{3,2,1,0:T(8,128)(2,1)S(1)}, u32[]{:S(2)}, u32[]{:S(2)}) collective-permute-start(bf16[2,2,128,512]{3,2,1,0:T(8,128)(2,1)S(1)} %get-tuple-element.117), channel_id=1, source_target_pairs={{0,64},{8,72},{16,80},{24,88},{32,96},{40,104},{48,112},{56,120},{... | collective-permute-start | bytes 1572872 | tf_op jit(solution)/shard_map/ppermute | solution.py:33
  44.4 0.6 collective-permute-start.11
  45.0 7.3 %shard_map.148.refs_1_ = f32[48,1536]{1,0:T(8,128)S(1)} custom-call(bf16[128,1536]{1,0:T(8,128)(2,1)S(1)} %get-tuple-element.53.refs_0_, f32[48,1536]{1,0:T(8,128)S(1)} %shard_map.147.refs_1_, bf16[192,1536]{1,0:T(8,128)(2,1)S(1)} %collective-permute-done.5.refs_2_.refs_11_), custom_call_target="tpu_custom_call", output_to_operand_aliasing={{}: (1, {})} | custom-call | flops 8493465600 | bytes 589824 | tf_op jit(solution)/shard_map/pallas_call | solution.py:153
  52.4 75.7 %shard_map.149 = bf16[8,32,704]{2,1,0:T(8,128)(2,1)} custom-call(bf16[128,1536]{1,0:T(8,128)(2,1)S(1)} %get-tuple-element.53.refs_0_, f32[48,1536]{1,0:T(8,128)S(1)} %shard_map.148.refs_1_, bf16[96,1536]{1,0:T(8,128)(2,1)S(1)} %convolution_convert_fusion.refs_0_.refs_2_, bf16[32,512]{1,0:T(8,128)(2,1)S(1)} %copy-done.10, ...), custom_call_target="tpu_custom_call" | custom-call | flops 8493465600 | bytes 589824 | tf_op jit(solution)/shard_map/pallas_call | solution.py:153
  128.1 6.9 %all-to-all-start = ((bf16[8,32,704]{2,1,0:T(8,128)(2,1)}), bf16[8,32,704]{2,1,0:T(8,128)(2,1)S(1)}, u32[]{:S(2)}, u32[]{:S(2)}) async-start(bf16[8,32,704]{2,1,0:T(8,128)(2,1)} %shard_map.149), calls=%async_computation | async-start | bytes 786432 | tf_op jit(solution)/shard_map/all_to_all | solution.py:28
  135.1 0.8 copy-done.17
  136.1 1.6 pad_maximum_fusion.lane_ref.in_lane.out_lane
  137.7 8.2 %all-to-all-done = bf16[8,32,704]{2,1,0:T(8,128)(2,1)S(1)} async-done(((bf16[8,32,704]{2,1,0:T(8,128)(2,1)}), bf16[8,32,704]{2,1,0:T(8,128)(2,1)S(1)}, u32[]{:S(2)}, u32[]{:S(2)}) %all-to-all-start) | async-done | bytes 360480 | tf_op jit(solution)/shard_map/all_to_all | solution.py:28
  145.9 1.3 multiply_reduce_fusion.2
  147.2 0.8 copy-done.13
  148.5 1.5 convolution_convert_fusion.1
  149.9 3.5 %all-to-all-start.1 = ((bf16[8,96,512]{2,1,0:T(8,128)(2,1)}), bf16[8,96,512]{2,1,0:T(8,128)(2,1)S(1)}, u32[]{:S(2)}, u32[]{:S(2)}) async-start(bf16[8,96,512]{2,1,0:T(8,128)(2,1)} %bitcast.115), calls=%async_computation.1 | async-start | bytes 1572864 | tf_op jit(solution)/shard_map/all_to_all | solution.py:28
  154.0 14.8 %all-to-all-done.1 = bf16[8,96,512]{2,1,0:T(8,128)(2,1)S(1)} async-done(((bf16[8,96,512]{2,1,0:T(8,128)(2,1)}), bf16[8,96,512]{2,1,0:T(8,128)(2,1)S(1)}, u32[]{:S(2)}, u32[]{:S(2)}) %all-to-all-start.1) | async-done | bytes 786464 | tf_op jit(solution)/shard_map/all_to_all | solution.py:28
  168.8 5.6 %shard_map.150 = bf16[768,512]{1,0:T(8,128)(2,1)S(1)} custom-call(bf16[768,512]{1,0:T(8,128)(2,1)S(1)} %bitcast.106, bf16[4,2,2,128,512]{4,3,2,1,0:T(8,128)(2,1)S(1)} %pad_maximum_fusion.lane_ref.in_lane.out_lane, bf16[4,2,2,128,512]{4,3,2,1,0:T(8,128)(2,1)} %collective-permute-done.12.partner_ref.in_partner.out_partner), custom_call_target="tpu_custom_call" | custom-call | flops 3221225472 | bytes 4194304 | tf_op jit(solution)/shard_map/pallas_call | solution.py:278
  174.4 0.9 copy-done.3
  175.3 4.4 %all-to-all-start.2 = ((bf16[8,96,512]{2,1,0:T(8,128)(2,1)}), bf16[8,96,512]{2,1,0:T(8,128)(2,1)}, u32[]{:S(2)}, u32[]{:S(2)}) async-start(bf16[8,96,512]{2,1,0:T(8,128)(2,1)} %bitcast.109), calls=%async_computation.2 | async-start | bytes 1572864 | tf_op jit(solution)/shard_map/all_to_all | solution.py:28
  179.8 1.1 eq.102
  181.2 6.7 %shard_map.151 = (bf16[2048,768]{1,0:T(8,128)(2,1)S(1)}, bf16[2048,768]{1,0:T(8,128)(2,1)S(1)}, bf16[2048,512]{1,0:T(8,128)(2,1)S(1)}, bf16[512,2048]{1,0:T(8,128)(2,1)S(1)}) custom-call(bf16[768,512]{1,0:T(8,128)(2,1)S(1)} %bitcast.107, bf16[4,2,2,128,512]{4,3,2,1,0:T(8,128)(2,1)S(1)} %pad_maximum_fusion.lane_ref.in_lane.out_lane, ...), custom_call_target="tpu_custom_call" | custom-call | flops 1610612736 | bytes 17825792 | tf_op jit(solution)/shard_map/pallas_call | solution.py:320
  188.0 1.4 copy-done.1
  189.3 1.6 copy-done.4
  191.0 1.7 copy-done.6
  192.6 1.4 copy-done.8
  194.2 1.8 fusion.37
  196.5 0.8 add_add_fusion
  197.8 0.5 mul.202
  198.8 0.8 fusion.5
  199.6 22.1 %all_to_all.25.refs_1_.refs_3_ = bf16[8,112,512]{2,1,0:T(8,128)(2,1)S(1)} all-to-all(bf16[8,112,512]{2,1,0:T(8,128)(2,1)S(1)} %bitcast.113), channel_id=1, replica_groups=mesh['blk'=16,'exp'=8] {'exp'}, dimensions={0} | all-to-all | bytes 1835008 | tf_op jit(solution)/shard_map/all_to_all | solution.py:28
  221.7 2.3 shard_map.152
  224.3 4.1 %shard_map.153 = (f32[4,2,128,512]{3,2,1,0:T(8,128)S(1)}, bf16[4,2,128,512]{3,2,1,0:T(8,128)(2,1)S(1)}, bf16[2048,768]{1,0:T(8,128)(2,1)S(1)}) custom-call(bf16[2048,768]{1,0:T(8,128)(2,1)S(1)} %copy-done.5, bf16[2048,512]{1,0:T(8,128)(2,1)S(1)} %copy-done.9, bf16[768,512]{1,0:T(8,128)(2,1)S(1)} %bitcast.108, bf16[8,112,512]{2,1,0:T(8,128)(2,1)S(1)} %all_to_all.25.refs_1_.refs_3_), custom_call_target="tpu_custom_call" | custom-call | flops 3221225472 | bytes 9437184 | tf_op jit(solution)/shard_map/pallas_call | solution.py:419
  229.1 2.1 collective-permute-done.13
  231.6 0.8 pad_maximum_fusion.3
  232.5 0.7 collective-permute-start.16
  233.2 1.8 fusion.72
  235.0 0.9 slice_bitcast_fusion.6
  235.9 4.1 %collective-permute-start.18 = (bf16[2,128,512]{2,1,0:T(8,128)(2,1)}, bf16[2,128,512]{2,1,0:T(8,128)(2,1)}, u32[]{:S(2)}, u32[]{:S(2)}) collective-permute-start(bf16[2,128,512]{2,1,0:T(8,128)(2,1)} %get-tuple-element.112), channel_id=1, source_target_pairs={{0,64},{8,72},{16,80},{24,88},{32,96},{40,104},{48,112},{56,120},{... | collective-permute-start | bytes 786440 | tf_op jit(solution)/shard_map/ppermute | solution.py:33
  239.9 0.6 collective-permute-start.19
  240.6 2.7 %shard_map.154 = bf16[768,512]{1,0:T(8,128)(2,1)} custom-call(bf16[2048,768]{1,0:T(8,128)(2,1)S(1)} %get-tuple-element.90.pre_grad_ref, bf16[512,2048]{1,0:T(8,128)(2,1)S(1)} %copy-done.2), custom_call_target="tpu_custom_call" | custom-call | flops 1572864 | bytes 393216 | tf_op jit(solution)/shard_map/pallas_call | solution.py:440
  243.3 3.5 %all-to-all-start.4 = ((bf16[8,96,512]{2,1,0:T(8,128)(2,1)}), bf16[8,96,512]{2,1,0:T(8,128)(2,1)S(1)}, u32[]{:S(2)}, u32[]{:S(2)}) async-start(bf16[8,96,512]{2,1,0:T(8,128)(2,1)} %bitcast.22), calls=%async_computation.4 | async-start | bytes 1572864 | tf_op jit(solution)/shard_map/all_to_all | solution.py:28
  247.3 1.1 slice.130
  248.7 0.7 add_convert_fusion
  249.5 4.1 %collective-permute-start.22 = (bf16[144,512]{1,0:T(8,128)(2,1)S(1)}, bf16[144,512]{1,0:T(8,128)(2,1)S(1)}, u32[]{:S(2)}, u32[]{:S(2)}) collective-permute-start(bf16[144,512]{1,0:T(8,128)(2,1)S(1)} %get-tuple-element.121), channel_id=1, source_target_pairs={{0,64},{8,72},{16,80},{24,88},{32,96},{40,104},{48,112},{56,120},{... | collective-permute-start | bytes 442376 | tf_op jit(solution)/shard_map/ppermute | solution.py:33
  253.6 0.6 collective-permute-start.23
  254.2 0.5 collective-permute-done.19
  254.8 1.4 bitcast_add_fusion
  256.2 1.4 collective-permute-start.20
  257.7 2.5 collective-permute-done.22
  260.2 2.1 collective-permute-done.23
  262.2 0.6 slice.172
  262.9 0.6 slice.173
  263.4 0.8 fusion.42
  264.2 0.7 fusion.40
  265.4 1.1 fusion.9
  (127 shorter events, 8.0 us)
Async XLA Ops:
  0.6 0.9 copy-start
  0.6 9.7 %copy-start.22 = (s32[192,2]{0,1:T(2,128)S(1)}, s32[192,2]{0,1:T(2,128)}, u32[]{:S(2)}) copy-start(s32[192,2]{0,1:T(2,128)} %param.18) | copy-start | bytes 4612
  0.7 11.3 %copy-start.20 = (bf16[1,128,512]{2,1,0:T(8,128)(2,1)S(1)}, bf16[1,128,512]{2,1,0:T(8,128)(2,1)}, u32[]{:S(2)}) copy-start(bf16[1,128,512]{2,1,0:T(8,128)(2,1)} %param.16) | copy-start | bytes 393220
  0.7 11.3 %copy-start.19 = (bf16[1,128,512]{2,1,0:T(8,128)(2,1)S(1)}, bf16[1,128,512]{2,1,0:T(8,128)(2,1)}, u32[]{:S(2)}) copy-start(bf16[1,128,512]{2,1,0:T(8,128)(2,1)} %param.17) | copy-start | bytes 393220
  3.6 8.4 %collective-permute-start = (bf16[64,1536]{1,0:T(8,128)(2,1)S(1)}, bf16[64,1536]{1,0:T(8,128)(2,1)S(1)}, u32[]{:S(2)}, u32[]{:S(2)}) collective-permute-start(bf16[64,1536]{1,0:T(8,128)(2,1)S(1)} %slice.148), channel_id=1, source_target_pairs={{0,8},{8,0},{16,24},{24,16},{32,40},{40,32},{48,56},{56,48},{64,72... | collective-permute-start | bytes 589832 | tf_op jit(solution)/shard_map/ppermute | solution.py:33
  3.7 13.4 %collective-permute-start.1 = (bf16[64,1536]{1,0:T(8,128)(2,1)S(1)}, bf16[64,1536]{1,0:T(8,128)(2,1)S(1)}, u32[]{:S(2)}, u32[]{:S(2)}) collective-permute-start(bf16[64,1536]{1,0:T(8,128)(2,1)S(1)} %slice.148), channel_id=1, source_target_pairs={{0,64},{8,72},{16,80},{24,88},{32,96},{40,104},{48,112},{56,120},{... | collective-permute-start | bytes 589832 | tf_op jit(solution)/shard_map/ppermute | solution.py:33
  7.7 9.7 %collective-permute-start.2 = (bf16[64,1536]{1,0:T(8,128)(2,1)S(1)}, bf16[64,1536]{1,0:T(8,128)(2,1)S(1)}, u32[]{:S(2)}, u32[]{:S(2)}) collective-permute-start(bf16[64,1536]{1,0:T(8,128)(2,1)S(1)} %slice.148), channel_id=1, source_target_pairs={{0,96},{8,104},{16,112},{24,120},{32,64},{40,72},{48,80},{56,88},{... | collective-permute-start | bytes 589832 | tf_op jit(solution)/shard_map/ppermute | solution.py:33
  8.4 9.8 %collective-permute-start.3 = (bf16[64,1536]{1,0:T(8,128)(2,1)S(1)}, bf16[64,1536]{1,0:T(8,128)(2,1)S(1)}, u32[]{:S(2)}, u32[]{:S(2)}) collective-permute-start(bf16[64,1536]{1,0:T(8,128)(2,1)S(1)} %slice.148), channel_id=1, source_target_pairs={{0,32},{8,40},{16,48},{24,56},{32,0},{40,8},{48,16},{56,24},{64,96... | collective-permute-start | bytes 589832 | tf_op jit(solution)/shard_map/ppermute | solution.py:33
  8.7 9.5 %collective-permute-start.4 = (bf16[64,1536]{1,0:T(8,128)(2,1)S(1)}, bf16[64,1536]{1,0:T(8,128)(2,1)S(1)}, u32[]{:S(2)}, u32[]{:S(2)}) collective-permute-start(bf16[64,1536]{1,0:T(8,128)(2,1)S(1)} %slice.148), channel_id=1, source_target_pairs={{0,16},{8,24},{16,0},{24,8},{32,48},{40,56},{48,32},{56,40},{64,80... | collective-permute-start | bytes 589832 | tf_op jit(solution)/shard_map/ppermute | solution.py:33
  18.3 11.5 %collective-permute-start.6 = (bf16[256,1536]{1,0:T(8,128)(2,1)S(1)}, bf16[256,1536]{1,0:T(8,128)(2,1)S(1)}, u32[]{:S(2)}, u32[]{:S(2)}) collective-permute-start(bf16[256,1536]{1,0:T(8,128)(2,1)S(1)} %pad_maximum_fusion.1), channel_id=1, source_target_pairs={{0,8},{8,0},{16,24},{24,16},{32,40},{40,32},{48,56},{56,48},{64,72... | collective-permute-start | bytes 2359304 | tf_op jit(solution)/shard_map/ppermute | solution.py:33
  18.4 21.7 %collective-permute-start.5 = (bf16[192,1536]{1,0:T(8,128)(2,1)S(1)}, bf16[192,1536]{1,0:T(8,128)(2,1)S(1)}, u32[]{:S(2)}, u32[]{:S(2)}) collective-permute-start(bf16[192,1536]{1,0:T(8,128)(2,1)S(1)} %pad_maximum_fusion.2), channel_id=1, source_target_pairs={{0,16},{8,24},{16,0},{24,8},{32,48},{40,56},{48,32},{56,40},{64,80... | collective-permute-start | bytes 1769480 | tf_op jit(solution)/shard_map/ppermute | solution.py:33
  29.8 10.3 %collective-permute-start.7 = (bf16[2,128,512]{2,1,0:T(8,128)(2,1)S(1)}, bf16[2,128,512]{2,1,0:T(8,128)(2,1)S(1)}, u32[]{:S(2)}, u32[]{:S(2)}) collective-permute-start(bf16[2,128,512]{2,1,0:T(8,128)(2,1)S(1)} %pad_maximum_fusion.5), channel_id=1, source_target_pairs={{0,16},{8,24},{16,0},{24,8},{32,48},{40,56},{48,32},{56,40},{64,80... | collective-permute-start | bytes 786440 | tf_op jit(solution)/shard_map/ppermute | solution.py:33
  40.2 12.2 %copy-start.10 = (bf16[32,512]{1,0:T(8,128)(2,1)S(1)}, bf16[32,512]{1,0:T(8,128)(2,1)}, u32[]{:S(2)}) copy-start(bf16[32,512]{1,0:T(8,128)(2,1)} %refs_3_.1) | copy-start | bytes 98308
  40.2 94.8 %collective-permute-start.9 = (bf16[2,2,128,512]{3,2,1,0:T(8,128)(2,1)S(1)}, bf16[2,2,128,512]{3,2,1,0:T(8,128)(2,1)S(1)}, u32[]{:S(2)}, u32[]{:S(2)}) collective-permute-start(bf16[2,2,128,512]{3,2,1,0:T(8,128)(2,1)S(1)} %get-tuple-element.117), channel_id=1, source_target_pairs={{0,32},{8,40},{16,48},{24,56},{32,0},{40,8},{48,16},{56,24},{64,96... | collective-permute-start | bytes 1572872 | tf_op jit(solution)/shard_map/ppermute | solution.py:33
  41.3 93.8 %collective-permute-start.10 = (bf16[2,2,128,512]{3,2,1,0:T(8,128)(2,1)S(1)}, bf16[2,2,128,512]{3,2,1,0:T(8,128)(2,1)S(1)}, u32[]{:S(2)}, u32[]{:S(2)}) collective-permute-start(bf16[2,2,128,512]{3,2,1,0:T(8,128)(2,1)S(1)} %get-tuple-element.117), channel_id=1, source_target_pairs={{0,64},{8,72},{16,80},{24,88},{32,96},{40,104},{48,112},{56,120},{... | collective-permute-start | bytes 1572872 | tf_op jit(solution)/shard_map/ppermute | solution.py:33
  44.4 90.7 %collective-permute-start.11 = (bf16[2,2,128,512]{3,2,1,0:T(8,128)(2,1)S(1)}, bf16[2,2,128,512]{3,2,1,0:T(8,128)(2,1)}, u32[]{:S(2)}, u32[]{:S(2)}) collective-permute-start(bf16[2,2,128,512]{3,2,1,0:T(8,128)(2,1)S(1)} %get-tuple-element.117), channel_id=1, source_target_pairs={{0,96},{8,104},{16,112},{24,120},{32,64},{40,72},{48,80},{56,88},{... | collective-permute-start | bytes 1572872 | tf_op jit(solution)/shard_map/ppermute | solution.py:33
  45.0 7.4 %collective-permute-start.8 = (bf16[192,1536]{1,0:T(8,128)(2,1)S(1)}, bf16[192,1536]{1,0:T(8,128)(2,1)S(1)}, u32[]{:S(2)}, u32[]{:S(2)}) collective-permute-start(bf16[192,1536]{1,0:T(8,128)(2,1)S(1)} %collective-permute-done.5.refs_2_.refs_11_), channel_id=1, source_target_pairs={{0,8},{8,0},{16,24},{24,16},{32,40},{40,32},{48,56},{56,48},{64,72... | collective-permute-start | bytes 1769480 | tf_op jit(solution)/shard_map/ppermute | solution.py:33
  128.1 17.8 %all-to-all-start = ((bf16[8,32,704]{2,1,0:T(8,128)(2,1)}), bf16[8,32,704]{2,1,0:T(8,128)(2,1)S(1)}, u32[]{:S(2)}, u32[]{:S(2)}) async-start(bf16[8,32,704]{2,1,0:T(8,128)(2,1)} %shard_map.149), calls=%async_computation | async-start | bytes 786432 | tf_op jit(solution)/shard_map/all_to_all | solution.py:28
  135.1 0.8 copy-start.17
  135.1 1.0 copy-start.18
  136.1 11.9 %copy-start.23 = (f32[512]{0:T(512)S(1)}, f32[512]{0:T(512)}, u32[]{:S(2)}) copy-start(f32[512]{0:T(512)} %param.14) | copy-start | bytes 6148
  145.9 22.9 %collective-permute-start.12 = (bf16[4,2,2,128,512]{4,3,2,1,0:T(8,128)(2,1)S(1)}, bf16[4,2,2,128,512]{4,3,2,1,0:T(8,128)(2,1)}, u32[]{:S(2)}, u32[]{:S(2)}) collective-permute-start(bf16[4,2,2,128,512]{4,3,2,1,0:T(8,128)(2,1)S(1)} %pad_maximum_fusion.lane_ref.in_lane.out_lane), channel_id=1, source_target_pairs={{0,8},{8,0},{16,24},{24,16},{32,40},{40,32},{48,56},{56,48},{64,72... | collective-permute-start | bytes 6291464 | tf_op jit(solution)/shard_map/ppermute | solution.py:33
  147.2 0.8 copy-start.13
  148.1 5.5 %copy-start.11 = (bf16[192,512]{1,0:T(8,128)(2,1)}, bf16[192,512]{1,0:T(8,128)(2,1)S(1)}, u32[]{:S(2)}) copy-start(bf16[192,512]{1,0:T(8,128)(2,1)S(1)} %multiply_convert_fusion.2) | copy-start | bytes 589828
  148.3 5.2 %copy-start.21 = (bf16[8,512]{1,0:T(8,128)(2,1)S(1)}, bf16[8,512]{1,0:T(8,128)(2,1)}, u32[]{:S(2)}) copy-start(bf16[8,512]{1,0:T(8,128)(2,1)} %param.13) | copy-start | bytes 24580
  149.9 18.8 %all-to-all-start.1 = ((bf16[8,96,512]{2,1,0:T(8,128)(2,1)}), bf16[8,96,512]{2,1,0:T(8,128)(2,1)S(1)}, u32[]{:S(2)}, u32[]{:S(2)}) async-start(bf16[8,96,512]{2,1,0:T(8,128)(2,1)} %bitcast.115), calls=%async_computation.1 | async-start | bytes 1572864 | tf_op jit(solution)/shard_map/all_to_all | solution.py:28
  174.4 0.9 copy-start.3
  175.3 18.9 %all-to-all-start.2 = ((bf16[8,96,512]{2,1,0:T(8,128)(2,1)}), bf16[8,96,512]{2,1,0:T(8,128)(2,1)}, u32[]{:S(2)}, u32[]{:S(2)}) async-start(bf16[8,96,512]{2,1,0:T(8,128)(2,1)} %bitcast.109), calls=%async_computation.2 | async-start | bytes 1572864 | tf_op jit(solution)/shard_map/all_to_all | solution.py:28
  187.9 1.4 copy-start.1
  189.3 1.6 copy-start.4
  191.0 1.7 copy-start.6
  192.6 1.4 copy-start.8
  194.0 2.0 copy-start.14
  194.2 2.1 copy-start.15
  194.2 2.1 copy-start.24
  197.5 0.9 copy-start.12
  198.8 22.9 %copy-start.7 = (bf16[2048,768]{1,0:T(8,128)(2,1)S(1)}, bf16[2048,768]{1,0:T(8,128)(2,1)}, u32[]{:S(2)}) copy-start(bf16[2048,768]{1,0:T(8,128)(2,1)} %copy-done.6) | copy-start | bytes 9437188
  221.7 2.4 copy-start.5
  221.7 2.5 copy-start.9
  224.1 7.1 %collective-permute-start.14 = (bf16[4,2,128,512]{3,2,1,0:T(8,128)(2,1)S(1)}, bf16[4,2,128,512]{3,2,1,0:T(8,128)(2,1)S(1)}, u32[]{:S(2)}, u32[]{:S(2)}) collective-permute-start(bf16[4,2,128,512]{3,2,1,0:T(8,128)(2,1)S(1)} %get-tuple-element.80), channel_id=1, source_target_pairs={{0,8},{8,0},{16,24},{24,16},{32,40},{40,32},{48,56},{56,48},{64,72... | collective-permute-start | bytes 3145736 | tf_op jit(solution)/shard_map/ppermute | solution.py:33
  228.4 4.8 %collective-permute-start.15 = (bf16[4,2,128,512]{3,2,1,0:T(8,128)(2,1)S(1)}, bf16[4,2,128,512]{3,2,1,0:T(8,128)(2,1)S(1)}, u32[]{:S(2)}, u32[]{:S(2)}) collective-permute-start(bf16[4,2,128,512]{3,2,1,0:T(8,128)(2,1)S(1)} %get-tuple-element.88), channel_id=1, source_target_pairs={{0,8},{8,0},{16,24},{24,16},{32,40},{40,32},{48,56},{56,48},{64,72... | collective-permute-start | bytes 3145736 | tf_op jit(solution)/shard_map/ppermute | solution.py:33
  228.8 2.3 collective-permute-start.13
  232.5 14.9 %collective-permute-start.16 = (bf16[528,512]{1,0:T(8,128)(2,1)}, bf16[528,512]{1,0:T(8,128)(2,1)}, u32[]{:S(2)}, u32[]{:S(2)}) collective-permute-start(bf16[528,512]{1,0:T(8,128)(2,1)} %pad_maximum_fusion.3), channel_id=1, source_target_pairs={{0,16},{8,24},{16,0},{24,8},{32,48},{40,56},{48,32},{56,40},{64,80... | collective-permute-start | bytes 1622024 | tf_op jit(solution)/shard_map/ppermute | solution.py:33
  233.2 7.4 %copy-start.2 = (bf16[512,2048]{1,0:T(8,128)(2,1)S(1)}, bf16[512,2048]{1,0:T(8,128)(2,1)}, u32[]{:S(2)}) copy-start(bf16[512,2048]{1,0:T(8,128)(2,1)} %copy-done.1) | copy-start | bytes 6291460
  235.9 17.8 %collective-permute-start.17 = (bf16[2,128,512]{2,1,0:T(8,128)(2,1)}, bf16[2,128,512]{2,1,0:T(8,128)(2,1)}, u32[]{:S(2)}, u32[]{:S(2)}) collective-permute-start(bf16[2,128,512]{2,1,0:T(8,128)(2,1)} %get-tuple-element.110), channel_id=1, source_target_pairs={{0,32},{8,40},{16,48},{24,56},{32,0},{40,8},{48,16},{56,24},{64,96... | collective-permute-start | bytes 786440 | tf_op jit(solution)/shard_map/ppermute | solution.py:33
  235.9 18.4 %collective-permute-start.18 = (bf16[2,128,512]{2,1,0:T(8,128)(2,1)}, bf16[2,128,512]{2,1,0:T(8,128)(2,1)}, u32[]{:S(2)}, u32[]{:S(2)}) collective-permute-start(bf16[2,128,512]{2,1,0:T(8,128)(2,1)} %get-tuple-element.112), channel_id=1, source_target_pairs={{0,64},{8,72},{16,80},{24,88},{32,96},{40,104},{48,112},{56,120},{... | collective-permute-start | bytes 786440 | tf_op jit(solution)/shard_map/ppermute | solution.py:33
  239.9 14.9 %collective-permute-start.19 = (bf16[2,128,512]{2,1,0:T(8,128)(2,1)}, bf16[2,128,512]{2,1,0:T(8,128)(2,1)}, u32[]{:S(2)}, u32[]{:S(2)}) collective-permute-start(bf16[2,128,512]{2,1,0:T(8,128)(2,1)} %get-tuple-element.111), channel_id=1, source_target_pairs={{0,96},{8,104},{16,112},{24,120},{32,64},{40,72},{48,80},{56,88},{... | collective-permute-start | bytes 786440 | tf_op jit(solution)/shard_map/ppermute | solution.py:33
  243.3 20.9 %all-to-all-start.4 = ((bf16[8,96,512]{2,1,0:T(8,128)(2,1)}), bf16[8,96,512]{2,1,0:T(8,128)(2,1)S(1)}, u32[]{:S(2)}, u32[]{:S(2)}) async-start(bf16[8,96,512]{2,1,0:T(8,128)(2,1)} %bitcast.22), calls=%async_computation.4 | async-start | bytes 1572864 | tf_op jit(solution)/shard_map/all_to_all | solution.py:28
  249.5 8.2 %collective-permute-start.21 = (bf16[144,512]{1,0:T(8,128)(2,1)S(1)}, bf16[144,512]{1,0:T(8,128)(2,1)S(1)}, u32[]{:S(2)}, u32[]{:S(2)}) collective-permute-start(bf16[144,512]{1,0:T(8,128)(2,1)S(1)} %get-tuple-element.120), channel_id=1, source_target_pairs={{0,32},{8,40},{16,48},{24,56},{32,0},{40,8},{48,16},{56,24},{64,96... | collective-permute-start | bytes 442376 | tf_op jit(solution)/shard_map/ppermute | solution.py:33
  249.5 10.6 %collective-permute-start.22 = (bf16[144,512]{1,0:T(8,128)(2,1)S(1)}, bf16[144,512]{1,0:T(8,128)(2,1)S(1)}, u32[]{:S(2)}, u32[]{:S(2)}) collective-permute-start(bf16[144,512]{1,0:T(8,128)(2,1)S(1)} %get-tuple-element.121), channel_id=1, source_target_pairs={{0,64},{8,72},{16,80},{24,88},{32,96},{40,104},{48,112},{56,120},{... | collective-permute-start | bytes 442376 | tf_op jit(solution)/shard_map/ppermute | solution.py:33
  253.6 11.3 %copy-start.16 = (pred[192,2,768]{2,1,0:T(4,128)(4,1)S(1)}, pred[192,2,768]{2,1,0:T(4,128)(4,1)}, u32[]{:S(2)}) copy-start(pred[192,2,768]{2,1,0:T(4,128)(4,1)} %eq.102) | copy-start | bytes 884740
  253.6 8.6 %collective-permute-start.23 = (bf16[144,512]{1,0:T(8,128)(2,1)S(1)}, bf16[144,512]{1,0:T(8,128)(2,1)S(1)}, u32[]{:S(2)}, u32[]{:S(2)}) collective-permute-start(bf16[144,512]{1,0:T(8,128)(2,1)S(1)} %get-tuple-element.122), channel_id=1, source_target_pairs={{0,96},{8,104},{16,112},{24,120},{32,64},{40,72},{48,80},{56,88},{... | collective-permute-start | bytes 442376 | tf_op jit(solution)/shard_map/ppermute | solution.py:33
  256.2 8.0 %collective-permute-start.20 = (bf16[128,512]{1,0:T(8,128)(2,1)S(1)}, bf16[128,512]{1,0:T(8,128)(2,1)S(1)}, u32[]{:S(2)}, u32[]{:S(2)}) collective-permute-start(bf16[128,512]{1,0:T(8,128)(2,1)S(1)} %fusion.45), channel_id=1, source_target_pairs={{0,16},{8,24},{16,0},{24,8},{32,48},{40,56},{48,32},{56,40},{64,80... | collective-permute-start | bytes 393224 | tf_op jit(solution)/shard_map/ppermute | solution.py:33

commit v3 on v2

--- a/solution.py
+++ b/solution.py
@@ -598,16 +598,16 @@
     row_grads = rows_back(pre_grad, in_weight)
     back_home = exchange(row_grads.reshape(experts, capacity, width))
     out_beside, in_sums = lax.optimization_barrier((out_beside, in_sums))
-    sum_rows = (
-        out_sent[-SUM_ROWS:].astype(jnp.float32) + out_beside[-SUM_ROWS:].astype(jnp.float32)
-    ).astype(jnp.bfloat16)
-    out_sums = out_sums[:, 0] + out_beside[:-SUM_ROWS].reshape(out_sums.shape[:1] + out_sums.shape[2:])
+    own = add_rows(out_sums[:, 0], out_sent[-SUM_ROWS:].astype(jnp.float32))
+    own = own + out_beside.astype(jnp.float32)
+    sum_rows = own[-SUM_ROWS:].astype(jnp.bfloat16)
+    out_sums = own[:-SUM_ROWS].reshape(out_sums.shape[0], -1, width)
     out_parts = [
         swap(add_rows(out_sums[d].astype(jnp.bfloat16), sum_rows), 4 * d) for d in (1, 2, 3)
     ]
-    expert_out_grads = add_swapped(out_sums[0], [part[:-SUM_ROWS] for part in out_parts])[None]
-    first, second, third = [part[-SUM_ROWS:].astype(jnp.float32) for part in out_parts]
-    sums = (sum_rows.astype(jnp.float32) + first) + (second + third)
+    first, second, third = [part.astype(jnp.float32) for part in out_parts]
+    totals = (add_rows(out_sums[0], sum_rows.astype(jnp.float32)) + first) + (second + third)
+    expert_out_grads, sums = totals[None, :-SUM_ROWS], totals[-SUM_ROWS:]
     router_grad, gain_grad = sums[:experts], sums[experts]
     in_sums = add_swapped(in_sums[0], in_parts)
     in_beside = swap(in_sums[1], 2)

time: 267 us -> 267 us (level)
    unnamed x51 -> x53, local copies, waits for them, and re-layouts: 9.9 us -> 9.92 us
  transfers between devices with their start and end apart: 28 -> 28, of which waited for: 10 -> 9; matrix products, arithmetic and copies ran while one was open for 7% -> 7% of each run, Pallas kernels for 45% -> 46%
where the time goes in v3:
time: 267 us; the launch traced here: 266 us
  Pallas kernels  129 us (48%)
  starting transfers between devices  44.8 us (17%)
  waiting for transfers between devices  30.9 us (12%)
  blocking collectives  22.2 us (8%)
  local copies, waits for them, and re-layouts  15.9 us (6%)
  other arithmetic  12.3 us (5%)
  matrix products  9.19 us (3%)
    pallas_call x5, Pallas kernels, attention_call(): pl.pallas_call(kernel, out_shape=out_shape, in_specs=specs * len(operands...  108 us
    ppermute x24, starting transfers between devices, hop(): lax.ppermute(value, axis, [(i, target(i) % count) for i in range(count)])  26.2 us
    all_to_all x4, waiting for transfers between devices, exchange(): lax.all_to_all(buffer, 'exp', split_axis=0, concat_axis=0, tiled=True)  23.1 us
    all_to_all x1, blocking collectives, exchange(): lax.all_to_all(buffer, 'exp', split_axis=0, concat_axis=0, tiled=True)  22.2 us
    all_to_all x4, starting transfers between devices, exchange(): lax.all_to_all(buffer, 'exp', split_axis=0, concat_axis=0, tiled=True)  18.6 us
    unnamed x53, local copies, waits for them, and re-layouts  9.92 us
    ppermute x24, waiting for transfers between devices, hop(): lax.ppermute(value, axis, [(i, target(i) % count) for i in range(count)])  7.81 us
    pallas_call x1, Pallas kernels, expert_slopes(): pl.pallas_call(expert_slopes_kernel, grid=(lane.shape[0],), out_shape=(ja...  6.75 us
  transfers between devices with their start and end apart: 28, of which 9 were waited for; matrix products, arithmetic and copies ran while one was open for 7% of the time, Pallas kernels for 46%

profile of v3, /device:TPU:0, one launch (start us, length us, event | category | flops | bytes accessed | tf_op | source)
XLA Modules:
  0.0 265.8 jit_solution(11310865557612840371)
XLA Ops:
  0.7 0.9 copy-done
  1.5 2.0 convolution_convert_fusion.refs_0_.refs_2_
  3.7 4.0 %collective-permute-start.1 = (bf16[64,1536]{1,0:T(8,128)(2,1)S(1)}, bf16[64,1536]{1,0:T(8,128)(2,1)S(1)}, u32[]{:S(2)}, u32[]{:S(2)}) collective-permute-start(bf16[64,1536]{1,0:T(8,128)(2,1)S(1)} %slice.138), channel_id=1, source_target_pairs={{0,64},{8,72},{16,80},{24,88},{32,96},{40,104},{48,112},{56,120},{... | collective-permute-start | bytes 589832 | tf_op jit(solution)/shard_map/ppermute | solution.py:33
  7.7 0.7 collective-permute-start.2
  8.7 1.6 collective-permute-start.4
  10.7 0.9 reduce-window.6
  12.0 5.0 %shard_map.145 = (bf16[128,1536]{1,0:T(8,128)(2,1)S(1)}, f32[48,1536]{1,0:T(8,128)S(1)}) custom-call(bf16[96,1536]{1,0:T(8,128)(2,1)S(1)} %convolution_convert_fusion.refs_0_.refs_2_, bf16[64,1536]{1,0:T(8,128)(2,1)S(1)} %collective-permute-done.refs_1_.refs_5_), custom_call_target="tpu_custom_call" | custom-call | flops 5662310400 | bytes 393216 | tf_op jit(solution)/shard_map/pallas_call | solution.py:153
  17.4 0.8 collective-permute-done.3.refs_4_.refs_8_
  18.4 1.7 collective-permute-start.5
  20.1 9.7 %shard_map.146.refs_1_ = f32[48,1536]{1,0:T(8,128)S(1)} custom-call(bf16[128,1536]{1,0:T(8,128)(2,1)S(1)} %get-tuple-element.53.refs_0_, f32[48,1536]{1,0:T(8,128)S(1)} %get-tuple-element.59.refs_1_, bf16[64,1536]{1,0:T(8,128)(2,1)S(1)} %collective-permute-done.1.refs_2_.refs_6_, ...), custom_call_target="tpu_custom_call", output_to_operand_aliasing={{}: (1, {})} | custom-call | flops 11324620800 | bytes 786432 | tf_op jit(solution)/shard_map/pallas_call | solution.py:153
  30.3 9.8 %shard_map.147.refs_1_ = f32[48,1536]{1,0:T(8,128)S(1)} custom-call(bf16[128,1536]{1,0:T(8,128)(2,1)S(1)} %get-tuple-element.53.refs_0_, f32[48,1536]{1,0:T(8,128)S(1)} %shard_map.146.refs_1_, bf16[256,1536]{1,0:T(8,128)(2,1)S(1)} %collective-permute-done.6.refs_2_.refs_10_), custom_call_target="tpu_custom_call", output_to_operand_aliasing={{}: (1, {})} | custom-call | flops 11324620800 | bytes 786432 | tf_op jit(solution)/shard_map/pallas_call | solution.py:153
  40.2 1.1 collective-permute-start.9
  41.3 3.1 %collective-permute-start.10 = (bf16[2,2,128,512]{3,2,1,0:T(8,128)(2,1)S(1)}, bf16[2,2,128,512]{3,2,1,0:T(8,128)(2,1)S(1)}, u32[]{:S(2)}, u32[]{:S(2)}) collective-permute-start(bf16[2,2,128,512]{3,2,1,0:T(8,128)(2,1)S(1)} %get-tuple-element.118), channel_id=1, source_target_pairs={{0,64},{8,72},{16,80},{24,88},{32,96},{40,104},{48,112},{56,120},{... | collective-permute-start | bytes 1572872 | tf_op jit(solution)/shard_map/ppermute | solution.py:33
  44.4 0.6 collective-permute-start.11
  45.0 7.3 %shard_map.148.refs_1_ = f32[48,1536]{1,0:T(8,128)S(1)} custom-call(bf16[128,1536]{1,0:T(8,128)(2,1)S(1)} %get-tuple-element.53.refs_0_, f32[48,1536]{1,0:T(8,128)S(1)} %shard_map.147.refs_1_, bf16[192,1536]{1,0:T(8,128)(2,1)S(1)} %collective-permute-done.5.refs_2_.refs_11_), custom_call_target="tpu_custom_call", output_to_operand_aliasing={{}: (1, {})} | custom-call | flops 8493465600 | bytes 589824 | tf_op jit(solution)/shard_map/pallas_call | solution.py:153
  52.4 75.7 %shard_map.149 = bf16[8,32,704]{2,1,0:T(8,128)(2,1)} custom-call(bf16[128,1536]{1,0:T(8,128)(2,1)S(1)} %get-tuple-element.53.refs_0_, f32[48,1536]{1,0:T(8,128)S(1)} %shard_map.148.refs_1_, bf16[96,1536]{1,0:T(8,128)(2,1)S(1)} %convolution_convert_fusion.refs_0_.refs_2_, bf16[32,512]{1,0:T(8,128)(2,1)S(1)} %copy-done.10, ...), custom_call_target="tpu_custom_call" | custom-call | flops 8493465600 | bytes 589824 | tf_op jit(solution)/shard_map/pallas_call | solution.py:153
  128.1 6.9 %all-to-all-start = ((bf16[8,32,704]{2,1,0:T(8,128)(2,1)}), bf16[8,32,704]{2,1,0:T(8,128)(2,1)S(1)}, u32[]{:S(2)}, u32[]{:S(2)}) async-start(bf16[8,32,704]{2,1,0:T(8,128)(2,1)} %shard_map.149), calls=%async_computation | async-start | bytes 786432 | tf_op jit(solution)/shard_map/all_to_all | solution.py:28
  135.1 0.7 copy-done.18
  136.0 1.6 pad_maximum_fusion.lane_ref.in_lane.out_lane
  137.7 8.2 %all-to-all-done = bf16[8,32,704]{2,1,0:T(8,128)(2,1)S(1)} async-done(((bf16[8,32,704]{2,1,0:T(8,128)(2,1)}), bf16[8,32,704]{2,1,0:T(8,128)(2,1)S(1)}, u32[]{:S(2)}, u32[]{:S(2)}) %all-to-all-start) | async-done | bytes 360480 | tf_op jit(solution)/shard_map/all_to_all | solution.py:28
  145.9 1.3 multiply_reduce_fusion.2
  147.2 0.8 copy-done.14
  148.4 1.5 convolution_convert_fusion.1
  149.9 3.5 %all-to-all-start.1 = ((bf16[8,96,512]{2,1,0:T(8,128)(2,1)}), bf16[8,96,512]{2,1,0:T(8,128)(2,1)S(1)}, u32[]{:S(2)}, u32[]{:S(2)}) async-start(bf16[8,96,512]{2,1,0:T(8,128)(2,1)} %bitcast.99), calls=%async_computation.1 | async-start | bytes 1572864 | tf_op jit(solution)/shard_map/all_to_all | solution.py:28
  154.0 14.8 %all-to-all-done.1 = bf16[8,96,512]{2,1,0:T(8,128)(2,1)S(1)} async-done(((bf16[8,96,512]{2,1,0:T(8,128)(2,1)}), bf16[8,96,512]{2,1,0:T(8,128)(2,1)S(1)}, u32[]{:S(2)}, u32[]{:S(2)}) %all-to-all-start.1) | async-done | bytes 786464 | tf_op jit(solution)/shard_map/all_to_all | solution.py:28
  168.7 5.6 %shard_map.150 = bf16[768,512]{1,0:T(8,128)(2,1)S(1)} custom-call(bf16[768,512]{1,0:T(8,128)(2,1)S(1)} %bitcast.90, bf16[4,2,2,128,512]{4,3,2,1,0:T(8,128)(2,1)S(1)} %pad_maximum_fusion.lane_ref.in_lane.out_lane, bf16[4,2,2,128,512]{4,3,2,1,0:T(8,128)(2,1)} %collective-permute-done.12.partner_ref.in_partner.out_partner), custom_call_target="tpu_custom_call" | custom-call | flops 3221225472 | bytes 4194304 | tf_op jit(solution)/shard_map/pallas_call | solution.py:278
  174.4 0.9 copy-done.3
  175.3 4.4 %all-to-all-start.2 = ((bf16[8,96,512]{2,1,0:T(8,128)(2,1)}), bf16[8,96,512]{2,1,0:T(8,128)(2,1)}, u32[]{:S(2)}, u32[]{:S(2)}) async-start(bf16[8,96,512]{2,1,0:T(8,128)(2,1)} %bitcast.93), calls=%async_computation.2 | async-start | bytes 1572864 | tf_op jit(solution)/shard_map/all_to_all | solution.py:28
  179.7 1.1 eq.102
  181.2 6.7 %shard_map.151 = (bf16[2048,768]{1,0:T(8,128)(2,1)S(1)}, bf16[2048,768]{1,0:T(8,128)(2,1)S(1)}, bf16[2048,512]{1,0:T(8,128)(2,1)S(1)}, bf16[512,2048]{1,0:T(8,128)(2,1)S(1)}) custom-call(bf16[768,512]{1,0:T(8,128)(2,1)S(1)} %bitcast.91, bf16[4,2,2,128,512]{4,3,2,1,0:T(8,128)(2,1)S(1)} %pad_maximum_fusion.lane_ref.in_lane.out_lane, ...), custom_call_target="tpu_custom_call" | custom-call | flops 1610612736 | bytes 17825792 | tf_op jit(solution)/shard_map/pallas_call | solution.py:320
  187.9 1.4 copy-done.1
  189.3 1.6 copy-done.4
  191.0 1.7 copy-done.6
  192.7 1.4 copy-done.8
  194.2 1.8 fusion.37
  196.5 0.8 add_add_fusion
  197.8 0.5 mul.202
  198.8 0.8 fusion.5
  199.5 22.2 %all_to_all.25.refs_1_.refs_3_ = bf16[8,112,512]{2,1,0:T(8,128)(2,1)S(1)} all-to-all(bf16[8,112,512]{2,1,0:T(8,128)(2,1)S(1)} %bitcast.97), channel_id=1, replica_groups=mesh['blk'=16,'exp'=8] {'exp'}, dimensions={0} | all-to-all | bytes 1835008 | tf_op jit(solution)/shard_map/all_to_all | solution.py:28
  221.8 2.3 shard_map.152
  224.3 4.1 %shard_map.153 = (f32[4,2,128,512]{3,2,1,0:T(8,128)S(1)}, bf16[4,2,128,512]{3,2,1,0:T(8,128)(2,1)S(1)}, bf16[2048,768]{1,0:T(8,128)(2,1)S(1)}) custom-call(bf16[2048,768]{1,0:T(8,128)(2,1)S(1)} %copy-done.5, bf16[2048,512]{1,0:T(8,128)(2,1)S(1)} %copy-done.9, bf16[768,512]{1,0:T(8,128)(2,1)S(1)} %bitcast.92, bf16[8,112,512]{2,1,0:T(8,128)(2,1)S(1)} %all_to_all.25.refs_1_.refs_3_), custom_call_target="tpu_custom_call" | custom-call | flops 3221225472 | bytes 9437184 | tf_op jit(solution)/shard_map/pallas_call | solution.py:419
  229.1 2.1 collective-permute-done.13
  231.7 1.0 pad_maximum_fusion.3
  232.6 0.7 collective-permute-start.16
  233.3 1.8 fusion.71
  235.1 0.9 slice_bitcast_fusion.6
  236.0 4.1 %collective-permute-start.18 = (bf16[2,128,512]{2,1,0:T(8,128)(2,1)}, bf16[2,128,512]{2,1,0:T(8,128)(2,1)}, u32[]{:S(2)}, u32[]{:S(2)}) collective-permute-start(bf16[2,128,512]{2,1,0:T(8,128)(2,1)} %get-tuple-element.112), channel_id=1, source_target_pairs={{0,64},{8,72},{16,80},{24,88},{32,96},{40,104},{48,112},{56,120},{... | collective-permute-start | bytes 786440 | tf_op jit(solution)/shard_map/ppermute | solution.py:33
  240.1 0.6 collective-permute-start.19
  240.7 2.8 %shard_map.154 = bf16[768,512]{1,0:T(8,128)(2,1)} custom-call(bf16[2048,768]{1,0:T(8,128)(2,1)S(1)} %get-tuple-element.90.pre_grad_ref, bf16[512,2048]{1,0:T(8,128)(2,1)S(1)} %copy-done.2), custom_call_target="tpu_custom_call" | custom-call | flops 1572864 | bytes 393216 | tf_op jit(solution)/shard_map/pallas_call | solution.py:440
  243.5 3.7 %all-to-all-start.4 = ((bf16[8,96,512]{2,1,0:T(8,128)(2,1)}), bf16[8,96,512]{2,1,0:T(8,128)(2,1)S(1)}, u32[]{:S(2)}, u32[]{:S(2)}) async-start(bf16[8,96,512]{2,1,0:T(8,128)(2,1)} %bitcast.22), calls=%async_computation.4 | async-start | bytes 1572864 | tf_op jit(solution)/shard_map/all_to_all | solution.py:28
  247.1 0.7 slice_convert_fusion.2
  247.9 1.2 fusion.70
  249.3 4.0 %collective-permute-start.22 = (bf16[144,512]{1,0:T(8,128)(2,1)S(1)}, bf16[144,512]{1,0:T(8,128)(2,1)S(1)}, u32[]{:S(2)}, u32[]{:S(2)}) collective-permute-start(bf16[144,512]{1,0:T(8,128)(2,1)S(1)} %get-tuple-element.122), channel_id=1, source_target_pairs={{0,64},{8,72},{16,80},{24,88},{32,96},{40,104},{48,112},{56,120},{... | collective-permute-start | bytes 442376 | tf_op jit(solution)/shard_map/ppermute | solution.py:33
  253.4 0.7 collective-permute-start.23
  254.1 0.8 collective-permute-done.19
  254.9 1.4 bitcast_add_fusion
  256.4 1.4 collective-permute-start.20
  257.8 1.7 collective-permute-done.22
  259.6 2.0 collective-permute-done.23
  261.6 0.6 slice.158
  262.2 0.6 slice.159
  262.8 0.7 slice_bitcast_fusion.3
  263.6 0.7 fusion.41
  264.8 1.1 fusion.9
  (133 shorter events, 7.4 us)
Async XLA Ops:
  0.6 0.9 copy-start
  0.6 9.7 %copy-start.23 = (s32[192,2]{0,1:T(2,128)S(1)}, s32[192,2]{0,1:T(2,128)}, u32[]{:S(2)}) copy-start(s32[192,2]{0,1:T(2,128)} %param.18) | copy-start | bytes 4612
  0.7 11.3 %copy-start.21 = (bf16[1,128,512]{2,1,0:T(8,128)(2,1)S(1)}, bf16[1,128,512]{2,1,0:T(8,128)(2,1)}, u32[]{:S(2)}) copy-start(bf16[1,128,512]{2,1,0:T(8,128)(2,1)} %param.16) | copy-start | bytes 393220
  0.7 11.3 %copy-start.20 = (bf16[1,128,512]{2,1,0:T(8,128)(2,1)S(1)}, bf16[1,128,512]{2,1,0:T(8,128)(2,1)}, u32[]{:S(2)}) copy-start(bf16[1,128,512]{2,1,0:T(8,128)(2,1)} %param.17) | copy-start | bytes 393220
  3.6 8.4 %collective-permute-start = (bf16[64,1536]{1,0:T(8,128)(2,1)S(1)}, bf16[64,1536]{1,0:T(8,128)(2,1)S(1)}, u32[]{:S(2)}, u32[]{:S(2)}) collective-permute-start(bf16[64,1536]{1,0:T(8,128)(2,1)S(1)} %slice.138), channel_id=1, source_target_pairs={{0,8},{8,0},{16,24},{24,16},{32,40},{40,32},{48,56},{56,48},{64,72... | collective-permute-start | bytes 589832 | tf_op jit(solution)/shard_map/ppermute | solution.py:33
  3.7 13.4 %collective-permute-start.1 = (bf16[64,1536]{1,0:T(8,128)(2,1)S(1)}, bf16[64,1536]{1,0:T(8,128)(2,1)S(1)}, u32[]{:S(2)}, u32[]{:S(2)}) collective-permute-start(bf16[64,1536]{1,0:T(8,128)(2,1)S(1)} %slice.138), channel_id=1, source_target_pairs={{0,64},{8,72},{16,80},{24,88},{32,96},{40,104},{48,112},{56,120},{... | collective-permute-start | bytes 589832 | tf_op jit(solution)/shard_map/ppermute | solution.py:33
  7.7 9.7 %collective-permute-start.2 = (bf16[64,1536]{1,0:T(8,128)(2,1)S(1)}, bf16[64,1536]{1,0:T(8,128)(2,1)S(1)}, u32[]{:S(2)}, u32[]{:S(2)}) collective-permute-start(bf16[64,1536]{1,0:T(8,128)(2,1)S(1)} %slice.138), channel_id=1, source_target_pairs={{0,96},{8,104},{16,112},{24,120},{32,64},{40,72},{48,80},{56,88},{... | collective-permute-start | bytes 589832 | tf_op jit(solution)/shard_map/ppermute | solution.py:33
  8.4 9.8 %collective-permute-start.3 = (bf16[64,1536]{1,0:T(8,128)(2,1)S(1)}, bf16[64,1536]{1,0:T(8,128)(2,1)S(1)}, u32[]{:S(2)}, u32[]{:S(2)}) collective-permute-start(bf16[64,1536]{1,0:T(8,128)(2,1)S(1)} %slice.138), channel_id=1, source_target_pairs={{0,32},{8,40},{16,48},{24,56},{32,0},{40,8},{48,16},{56,24},{64,96... | collective-permute-start | bytes 589832 | tf_op jit(solution)/shard_map/ppermute | solution.py:33
  8.7 9.5 %collective-permute-start.4 = (bf16[64,1536]{1,0:T(8,128)(2,1)S(1)}, bf16[64,1536]{1,0:T(8,128)(2,1)S(1)}, u32[]{:S(2)}, u32[]{:S(2)}) collective-permute-start(bf16[64,1536]{1,0:T(8,128)(2,1)S(1)} %slice.138), channel_id=1, source_target_pairs={{0,16},{8,24},{16,0},{24,8},{32,48},{40,56},{48,32},{56,40},{64,80... | collective-permute-start | bytes 589832 | tf_op jit(solution)/shard_map/ppermute | solution.py:33
  18.3 11.5 %collective-permute-start.6 = (bf16[256,1536]{1,0:T(8,128)(2,1)S(1)}, bf16[256,1536]{1,0:T(8,128)(2,1)S(1)}, u32[]{:S(2)}, u32[]{:S(2)}) collective-permute-start(bf16[256,1536]{1,0:T(8,128)(2,1)S(1)} %pad_maximum_fusion.1), channel_id=1, source_target_pairs={{0,8},{8,0},{16,24},{24,16},{32,40},{40,32},{48,56},{56,48},{64,72... | collective-permute-start | bytes 2359304 | tf_op jit(solution)/shard_map/ppermute | solution.py:33
  18.4 21.7 %collective-permute-start.5 = (bf16[192,1536]{1,0:T(8,128)(2,1)S(1)}, bf16[192,1536]{1,0:T(8,128)(2,1)S(1)}, u32[]{:S(2)}, u32[]{:S(2)}) collective-permute-start(bf16[192,1536]{1,0:T(8,128)(2,1)S(1)} %pad_maximum_fusion.2), channel_id=1, source_target_pairs={{0,16},{8,24},{16,0},{24,8},{32,48},{40,56},{48,32},{56,40},{64,80... | collective-permute-start | bytes 1769480 | tf_op jit(solution)/shard_map/ppermute | solution.py:33
  29.8 10.3 %collective-permute-start.7 = (bf16[2,128,512]{2,1,0:T(8,128)(2,1)S(1)}, bf16[2,128,512]{2,1,0:T(8,128)(2,1)S(1)}, u32[]{:S(2)}, u32[]{:S(2)}) collective-permute-start(bf16[2,128,512]{2,1,0:T(8,128)(2,1)S(1)} %pad_maximum_fusion.5), channel_id=1, source_target_pairs={{0,16},{8,24},{16,0},{24,8},{32,48},{40,56},{48,32},{56,40},{64,80... | collective-permute-start | bytes 786440 | tf_op jit(solution)/shard_map/ppermute | solution.py:33
  40.2 12.2 %copy-start.10 = (bf16[32,512]{1,0:T(8,128)(2,1)S(1)}, bf16[32,512]{1,0:T(8,128)(2,1)}, u32[]{:S(2)}) copy-start(bf16[32,512]{1,0:T(8,128)(2,1)} %refs_3_.1) | copy-start | bytes 98308
  40.2 94.8 %collective-permute-start.9 = (bf16[2,2,128,512]{3,2,1,0:T(8,128)(2,1)S(1)}, bf16[2,2,128,512]{3,2,1,0:T(8,128)(2,1)S(1)}, u32[]{:S(2)}, u32[]{:S(2)}) collective-permute-start(bf16[2,2,128,512]{3,2,1,0:T(8,128)(2,1)S(1)} %get-tuple-element.118), channel_id=1, source_target_pairs={{0,32},{8,40},{16,48},{24,56},{32,0},{40,8},{48,16},{56,24},{64,96... | collective-permute-start | bytes 1572872 | tf_op jit(solution)/shard_map/ppermute | solution.py:33
  41.3 93.7 %collective-permute-start.10 = (bf16[2,2,128,512]{3,2,1,0:T(8,128)(2,1)S(1)}, bf16[2,2,128,512]{3,2,1,0:T(8,128)(2,1)S(1)}, u32[]{:S(2)}, u32[]{:S(2)}) collective-permute-start(bf16[2,2,128,512]{3,2,1,0:T(8,128)(2,1)S(1)} %get-tuple-element.118), channel_id=1, source_target_pairs={{0,64},{8,72},{16,80},{24,88},{32,96},{40,104},{48,112},{56,120},{... | collective-permute-start | bytes 1572872 | tf_op jit(solution)/shard_map/ppermute | solution.py:33
  44.4 90.7 %collective-permute-start.11 = (bf16[2,2,128,512]{3,2,1,0:T(8,128)(2,1)S(1)}, bf16[2,2,128,512]{3,2,1,0:T(8,128)(2,1)}, u32[]{:S(2)}, u32[]{:S(2)}) collective-permute-start(bf16[2,2,128,512]{3,2,1,0:T(8,128)(2,1)S(1)} %get-tuple-element.118), channel_id=1, source_target_pairs={{0,96},{8,104},{16,112},{24,120},{32,64},{40,72},{48,80},{56,88},{... | collective-permute-start | bytes 1572872 | tf_op jit(solution)/shard_map/ppermute | solution.py:33
  45.0 7.4 %collective-permute-start.8 = (bf16[192,1536]{1,0:T(8,128)(2,1)S(1)}, bf16[192,1536]{1,0:T(8,128)(2,1)S(1)}, u32[]{:S(2)}, u32[]{:S(2)}) collective-permute-start(bf16[192,1536]{1,0:T(8,128)(2,1)S(1)} %collective-permute-done.5.refs_2_.refs_11_), channel_id=1, source_target_pairs={{0,8},{8,0},{16,24},{24,16},{32,40},{40,32},{48,56},{56,48},{64,72... | collective-permute-start | bytes 1769480 | tf_op jit(solution)/shard_map/ppermute | solution.py:33
  128.1 17.8 %all-to-all-start = ((bf16[8,32,704]{2,1,0:T(8,128)(2,1)}), bf16[8,32,704]{2,1,0:T(8,128)(2,1)S(1)}, u32[]{:S(2)}, u32[]{:S(2)}) async-start(bf16[8,32,704]{2,1,0:T(8,128)(2,1)} %shard_map.149), calls=%async_computation | async-start | bytes 786432 | tf_op jit(solution)/shard_map/all_to_all | solution.py:28
  135.0 0.8 copy-start.18
  135.1 1.0 copy-start.19
  136.0 11.9 %copy-start.24 = (f32[512]{0:T(512)S(1)}, f32[512]{0:T(512)}, u32[]{:S(2)}) copy-start(f32[512]{0:T(512)} %param.14) | copy-start | bytes 6148
  145.9 22.9 %collective-permute-start.12 = (bf16[4,2,2,128,512]{4,3,2,1,0:T(8,128)(2,1)S(1)}, bf16[4,2,2,128,512]{4,3,2,1,0:T(8,128)(2,1)}, u32[]{:S(2)}, u32[]{:S(2)}) collective-permute-start(bf16[4,2,2,128,512]{4,3,2,1,0:T(8,128)(2,1)S(1)} %pad_maximum_fusion.lane_ref.in_lane.out_lane), channel_id=1, source_target_pairs={{0,8},{8,0},{16,24},{24,16},{32,40},{40,32},{48,56},{56,48},{64,72... | collective-permute-start | bytes 6291464 | tf_op jit(solution)/shard_map/ppermute | solution.py:33
  147.2 0.8 copy-start.14
  148.0 5.5 %copy-start.12 = (bf16[192,512]{1,0:T(8,128)(2,1)}, bf16[192,512]{1,0:T(8,128)(2,1)S(1)}, u32[]{:S(2)}) copy-start(bf16[192,512]{1,0:T(8,128)(2,1)S(1)} %multiply_convert_fusion.2) | copy-start | bytes 589828
  148.4 5.1 %copy-start.22 = (bf16[8,512]{1,0:T(8,128)(2,1)S(1)}, bf16[8,512]{1,0:T(8,128)(2,1)}, u32[]{:S(2)}) copy-start(bf16[8,512]{1,0:T(8,128)(2,1)} %param.13) | copy-start | bytes 24580
  149.9 18.8 %all-to-all-start.1 = ((bf16[8,96,512]{2,1,0:T(8,128)(2,1)}), bf16[8,96,512]{2,1,0:T(8,128)(2,1)S(1)}, u32[]{:S(2)}, u32[]{:S(2)}) async-start(bf16[8,96,512]{2,1,0:T(8,128)(2,1)} %bitcast.99), calls=%async_computation.1 | async-start | bytes 1572864 | tf_op jit(solution)/shard_map/all_to_all | solution.py:28
  174.4 0.9 copy-start.3
  175.3 18.9 %all-to-all-start.2 = ((bf16[8,96,512]{2,1,0:T(8,128)(2,1)}), bf16[8,96,512]{2,1,0:T(8,128)(2,1)}, u32[]{:S(2)}, u32[]{:S(2)}) async-start(bf16[8,96,512]{2,1,0:T(8,128)(2,1)} %bitcast.93), calls=%async_computation.2 | async-start | bytes 1572864 | tf_op jit(solution)/shard_map/all_to_all | solution.py:28
  187.9 1.4 copy-start.1
  189.3 1.6 copy-start.4
  191.0 1.7 copy-start.6
  192.7 1.4 copy-start.8
  194.0 2.0 copy-start.15
  194.2 2.1 copy-start.16
  194.2 2.1 copy-start.25
  197.5 0.9 copy-start.13
  198.8 23.0 %copy-start.7 = (bf16[2048,768]{1,0:T(8,128)(2,1)S(1)}, bf16[2048,768]{1,0:T(8,128)(2,1)}, u32[]{:S(2)}) copy-start(bf16[2048,768]{1,0:T(8,128)(2,1)} %copy-done.6) | copy-start | bytes 9437188
  221.8 2.4 copy-start.5
  221.8 2.5 copy-start.9
  224.1 7.1 %collective-permute-start.14 = (bf16[4,2,128,512]{3,2,1,0:T(8,128)(2,1)S(1)}, bf16[4,2,128,512]{3,2,1,0:T(8,128)(2,1)S(1)}, u32[]{:S(2)}, u32[]{:S(2)}) collective-permute-start(bf16[4,2,128,512]{3,2,1,0:T(8,128)(2,1)S(1)} %get-tuple-element.80), channel_id=1, source_target_pairs={{0,8},{8,0},{16,24},{24,16},{32,40},{40,32},{48,56},{56,48},{64,72... | collective-permute-start | bytes 3145736 | tf_op jit(solution)/shard_map/ppermute | solution.py:33
  228.4 4.9 %collective-permute-start.15 = (bf16[4,2,128,512]{3,2,1,0:T(8,128)(2,1)S(1)}, bf16[4,2,128,512]{3,2,1,0:T(8,128)(2,1)S(1)}, u32[]{:S(2)}, u32[]{:S(2)}) collective-permute-start(bf16[4,2,128,512]{3,2,1,0:T(8,128)(2,1)S(1)} %get-tuple-element.88), channel_id=1, source_target_pairs={{0,8},{8,0},{16,24},{24,16},{32,40},{40,32},{48,56},{56,48},{64,72... | collective-permute-start | bytes 3145736 | tf_op jit(solution)/shard_map/ppermute | solution.py:33
  228.9 2.3 collective-permute-start.13
  231.6 3.6 %copy-start.11 = (f32[4,2,128,512]{3,2,1,0:T(8,128)}, f32[4,2,128,512]{3,2,1,0:T(8,128)S(1)}, u32[]{:S(2)}) copy-start(f32[4,2,128,512]{3,2,1,0:T(8,128)S(1)} %convert_add_fusion.1) | copy-start | bytes 6291460
  232.6 15.2 %collective-permute-start.16 = (bf16[528,512]{1,0:T(8,128)(2,1)}, bf16[528,512]{1,0:T(8,128)(2,1)}, u32[]{:S(2)}, u32[]{:S(2)}) collective-permute-start(bf16[528,512]{1,0:T(8,128)(2,1)} %pad_maximum_fusion.3), channel_id=1, source_target_pairs={{0,16},{8,24},{16,0},{24,8},{32,48},{40,56},{48,32},{56,40},{64,80... | collective-permute-start | bytes 1622024 | tf_op jit(solution)/shard_map/ppermute | solution.py:33
  235.1 5.6 %copy-start.2 = (bf16[512,2048]{1,0:T(8,128)(2,1)S(1)}, bf16[512,2048]{1,0:T(8,128)(2,1)}, u32[]{:S(2)}) copy-start(bf16[512,2048]{1,0:T(8,128)(2,1)} %copy-done.1) | copy-start | bytes 6291460
  236.0 17.4 %collective-permute-start.17 = (bf16[2,128,512]{2,1,0:T(8,128)(2,1)}, bf16[2,128,512]{2,1,0:T(8,128)(2,1)}, u32[]{:S(2)}, u32[]{:S(2)}) collective-permute-start(bf16[2,128,512]{2,1,0:T(8,128)(2,1)} %get-tuple-element.110), channel_id=1, source_target_pairs={{0,32},{8,40},{16,48},{24,56},{32,0},{40,8},{48,16},{56,24},{64,96... | collective-permute-start | bytes 786440 | tf_op jit(solution)/shard_map/ppermute | solution.py:33
  236.0 18.1 %collective-permute-start.18 = (bf16[2,128,512]{2,1,0:T(8,128)(2,1)}, bf16[2,128,512]{2,1,0:T(8,128)(2,1)}, u32[]{:S(2)}, u32[]{:S(2)}) collective-permute-start(bf16[2,128,512]{2,1,0:T(8,128)(2,1)} %get-tuple-element.112), channel_id=1, source_target_pairs={{0,64},{8,72},{16,80},{24,88},{32,96},{40,104},{48,112},{56,120},{... | collective-permute-start | bytes 786440 | tf_op jit(solution)/shard_map/ppermute | solution.py:33
  240.1 14.9 %collective-permute-start.19 = (bf16[2,128,512]{2,1,0:T(8,128)(2,1)}, bf16[2,128,512]{2,1,0:T(8,128)(2,1)}, u32[]{:S(2)}, u32[]{:S(2)}) collective-permute-start(bf16[2,128,512]{2,1,0:T(8,128)(2,1)} %get-tuple-element.111), channel_id=1, source_target_pairs={{0,96},{8,104},{16,112},{24,120},{32,64},{40,72},{48,80},{56,88},{... | collective-permute-start | bytes 786440 | tf_op jit(solution)/shard_map/ppermute | solution.py:33
  243.5 4.4 %slice-start = ((f32[4,2,128,512]{3,2,1,0:T(8,128)}), f32[4,1,128,512]{3,2,1,0:T(8,128)S(1)}, s32[]{:S(2)}) async-start(f32[4,2,128,512]{3,2,1,0:T(8,128)} %copy-done.11), calls=%async_computation.5 | async-start | bytes 2097152 | tf_op jit(solution)/shard_map/slice | solution.py:601
  243.5 20.1 %all-to-all-start.4 = ((bf16[8,96,512]{2,1,0:T(8,128)(2,1)}), bf16[8,96,512]{2,1,0:T(8,128)(2,1)S(1)}, u32[]{:S(2)}, u32[]{:S(2)}) async-start(bf16[8,96,512]{2,1,0:T(8,128)(2,1)} %bitcast.22), calls=%async_computation.4 | async-start | bytes 1572864 | tf_op jit(solution)/shard_map/all_to_all | solution.py:28
  249.2 8.6 %collective-permute-start.21 = (bf16[144,512]{1,0:T(8,128)(2,1)S(1)}, bf16[144,512]{1,0:T(8,128)(2,1)S(1)}, u32[]{:S(2)}, u32[]{:S(2)}) collective-permute-start(bf16[144,512]{1,0:T(8,128)(2,1)S(1)} %get-tuple-element.121), channel_id=1, source_target_pairs={{0,32},{8,40},{16,48},{24,56},{32,0},{40,8},{48,16},{56,24},{64,96... | collective-permute-start | bytes 442376 | tf_op jit(solution)/shard_map/ppermute | solution.py:33
  249.3 10.2 %collective-permute-start.22 = (bf16[144,512]{1,0:T(8,128)(2,1)S(1)}, bf16[144,512]{1,0:T(8,128)(2,1)S(1)}, u32[]{:S(2)}, u32[]{:S(2)}) collective-permute-start(bf16[144,512]{1,0:T(8,128)(2,1)S(1)} %get-tuple-element.122), channel_id=1, source_target_pairs={{0,64},{8,72},{16,80},{24,88},{32,96},{40,104},{48,112},{56,120},{... | collective-permute-start | bytes 442376 | tf_op jit(solution)/shard_map/ppermute | solution.py:33
  253.4 8.2 %collective-permute-start.23 = (bf16[144,512]{1,0:T(8,128)(2,1)S(1)}, bf16[144,512]{1,0:T(8,128)(2,1)S(1)}, u32[]{:S(2)}, u32[]{:S(2)}) collective-permute-start(bf16[144,512]{1,0:T(8,128)(2,1)S(1)} %slice.153), channel_id=1, source_target_pairs={{0,96},{8,104},{16,112},{24,120},{32,64},{40,72},{48,80},{56,88},{... | collective-permute-start | bytes 442376 | tf_op jit(solution)/shard_map/ppermute | solution.py:33
  256.4 7.9 %copy-start.17 = (pred[192,2,768]{2,1,0:T(4,128)(4,1)S(1)}, pred[192,2,768]{2,1,0:T(4,128)(4,1)}, u32[]{:S(2)}) copy-start(pred[192,2,768]{2,1,0:T(4,128)(4,1)} %eq.102) | copy-start | bytes 884740
  256.4 7.2 %collective-permute-start.20 = (bf16[128,512]{1,0:T(8,128)(2,1)S(1)}, bf16[128,512]{1,0:T(8,128)(2,1)S(1)}, u32[]{:S(2)}, u32[]{:S(2)}) collective-permute-start(bf16[128,512]{1,0:T(8,128)(2,1)S(1)} %fusion.44), channel_id=1, source_target_pairs={{0,16},{8,24},{16,0},{24,8},{32,48},{40,56},{48,32},{56,40},{64,80... | collective-permute-start | bytes 393224 | tf_op jit(solution)/shard_map/ppermute | solution.py:33
